TPU v7x, 256 devices: a whole 4x4x8 slice. The times are simulated.
256 devices in a mesh: seq: 32 (over y_lo, z, core), chan: 8 (over x, y_hi).
Axes of the slice: x: 4, y: 4 (y_hi: 2, y_lo: 2; y = y_hi * 2 + y_lo), z: 8, core: 2. Of those that a mesh axis runs over, the one named last changes fastest.
Arguments:
- tokens: bfloat16 [4096, 4096], P('seq', 'chan'), may hold values from -6 to 6
- w_in: bfloat16 [4096, 3, 2048], P(None, None, 'chan'), may hold values from -0.09375 to 0.09375
- short_taps: float32 [3, 3, 2048], P(None, None, 'chan'), may hold values from -3 to 3
- skip_gain: float32 [2048], P('chan'), may hold values from 0.5 to 1.5
- filters: float32 [128, 4096], P('chan'), may hold values from -4 to 4
- w_out: bfloat16 [2048, 4096], P('chan'), may hold values from -0.125 to 0.125
Outputs:
- mixed: bfloat16 [4096, 4096], P('seq', 'chan')
All inputs are finite; a program needn't handle non-finite values.
Results may differ from a plain program's by a relative error of at most 0.015.
Values may be sent and summed in bfloat16 or wider, within the bound.
No kernel may reach another device: no remote copies, remote signals or barrier semaphores. Data moves between devices by JAX's collectives and lax.ppermute only.
A program may use at most 64 MiB of HBM per device.

v0:
```python
import functools

import jax
import jax.numpy as jnp
from jax import lax
from jax.experimental import pallas as pl
from jax.experimental.pallas import tpu as pltpu
from jax.sharding import Mesh, PartitionSpec as P


SEQ = ("yl", "z", "core")
CHAN = ("x", "yh")
SPLIT = (2, 8, 2, 4, 2)
VMEM = pl.BlockSpec(memory_space=pltpu.VMEM)
SPACE = {"s": pltpu.SMEM, "v": pltpu.VMEM, "a": pl.ANY, "h": pltpu.HBM}
MIB = 1 << 20


def chan_shift(block, dx, dy):
    nx, ny = lax.axis_size("x"), lax.axis_size("yh")
    pairs = []
    for x in range(nx):
        for y in range(ny):
            pairs.append((x * ny + y, (x + dx) % nx * ny + (y + dy) % ny))
    return lax.ppermute(block, CHAN, pairs)


def call(body, out_shape, args, spaces, scratch=(), vmem=16, flops=1, nbytes=1):
    many = isinstance(out_shape, (tuple, list))
    return pl.pallas_call(
        body,
        out_shape=out_shape,
        in_specs=[pl.BlockSpec(memory_space=SPACE[c]) for c in spaces] + [VMEM] * (len(args) - len(spaces)),
        out_specs=[VMEM] * len(out_shape) if many else VMEM,
        scratch_shapes=list(scratch),
        compiler_params=pltpu.CompilerParams(vmem_limit_bytes=vmem * MIB),
        cost_estimate=pl.CostEstimate(flops=flops, bytes_accessed=nbytes, transcendentals=0),
    )(*args)


def prepare_body(own_ref, filters_ref, taps_ref, gain_ref, lags_ref, short_ref, skip_ref):
    own, group = own_ref[0], own_ref[1]
    size = lags_ref.shape[1]
    count = lags_ref.shape[0] // size
    before = jnp.zeros((size, size), jnp.float32)
    line = filters_ref[pl.ds(group, 1), :].astype(jnp.bfloat16).astype(jnp.float32)
    for k in range(count):
        here = jnp.broadcast_to(line[:, k * size : (k + 1) * size], (size, size))
        both = jnp.concatenate([before, here], axis=1)
        turned = pltpu.roll(both, 0, 1, stride=1, stride_axis=0)
        lags_ref[k * size : (k + 1) * size, :] = turned[:, size:].astype(jnp.bfloat16)
        before = here
    per, width = short_ref.shape[2], taps_ref.shape[2]
    lane = lax.broadcasted_iota(jnp.int32, (per, width), 1)
    row = lax.broadcasted_iota(jnp.int32, (per, width), 0)
    mine = lane == own + row

    def spread(v):
        picked = jnp.where(mine, jnp.broadcast_to(v, (per, width)), 0.0)
        return jnp.broadcast_to(jnp.sum(picked, axis=1, keepdims=True), (per, size))

    for j in range(taps_ref.shape[0]):
        for k in range(taps_ref.shape[1]):
            short_ref[j, k] = spread(taps_ref[j, k : k + 1, :])
    skip_ref[...] = spread(gain_ref[...])


def fetch(order, skip, w_hbm, into, sem):
    feats = into.shape[2]
    loads = []
    for i in range(into.shape[0]):
        start = pl.multiple_of(order[skip + i] * feats, feats)
        loads.append(pltpu.make_async_copy(w_hbm.at[:, pl.ds(start, feats)], into.at[i], sem.at[i]))
        loads[-1].start()
    return loads


def project_first_body(order, w_hbm, *refs):
    blocks, (out_ref, next_ref, w_ref, sem, next_sem) = refs[:-5], refs[-5:]
    count = len(blocks)
    loads = fetch(order, 0, w_hbm, w_ref, sem)
    later = fetch(order, count, w_hbm, next_ref, next_sem)
    for i, block in enumerate(blocks):
        loads[i].wait()
        for k in range(w_ref.shape[1]):
            part = jnp.dot(block[...], w_ref[i, k], preferred_element_type=jnp.float32)
            out_ref[k] = part if i == 0 else out_ref[k] + part
    for load in later:
        load.wait()


def project_near_body(skip, order, w_hbm, w_ref, *refs):
    blocks, (before_ref, out_ref, next_ref, next_sem) = refs[:-4], refs[-4:]
    later = fetch(order, skip, w_hbm, next_ref, next_sem)
    for k in range(w_ref.shape[1]):
        total = before_ref[k]
        for i, block in enumerate(blocks):
            total = total + jnp.dot(block[...], w_ref[i, k], preferred_element_type=jnp.float32)
        out_ref[k] = total
    for load in later:
        load.wait()


def project_far_body(w_ref, *refs):
    blocks, (before_ref, out_ref) = refs[:-2], refs[-2:]
    for k in range(w_ref.shape[1]):
        total = before_ref[k]
        for i, block in enumerate(blocks):
            total = total + jnp.dot(block[...], w_ref[i, k], preferred_element_type=jnp.float32)
        turned = total.T.reshape(out_ref.shape[0], out_ref.shape[2], out_ref.shape[3])
        out_ref[:, k] = turned.astype(jnp.bfloat16)


def mix_body(proj_ref, short_ref, gain_ref, lags_ref, out_ref, acc_ref):
    count, _, width, size = proj_ref.shape
    rows = count * width
    lane = lax.broadcasted_iota(jnp.int32, (rows, size), 1)

    def spread(v):
        return jnp.broadcast_to(v[None], (count, width, size)).reshape(rows, size)

    def stream(k):
        here = proj_ref[:, k].astype(jnp.float32).reshape(rows, size)
        before = jnp.concatenate([jnp.zeros((width, size), jnp.float32), here[: rows - width]], axis=0)
        total = spread(short_ref[0, k]) * here
        for j in (1, 2):
            moved = jnp.where(lane < j, pltpu.roll(before, j, 1), pltpu.roll(here, j, 1))
            total = total + spread(short_ref[j, k]) * moved
        return total

    gated = (stream(1) * stream(2)).astype(jnp.bfloat16)
    wide = gated.astype(jnp.float32)
    late = jnp.concatenate([jnp.zeros((width, size), jnp.float32), wide[: rows - width]], axis=0)
    pair = jnp.concatenate([gated, late.astype(jnp.bfloat16)], axis=1)
    acc_ref[...] = spread(gain_ref[...]) * wide
    for m in range(count // 2):
        skip = 2 * width * m
        acc_ref[skip:, :] += jnp.dot(
            pair[: rows - skip],
            lags_ref[2 * size * m : 2 * size * (m + 1), :],
            preferred_element_type=jnp.float32,
        )
    mixed = stream(0) * acc_ref[...]
    out_ref[...] = mixed.reshape(count, width, size).astype(jnp.bfloat16)


def output_body(target, mixer_ref, w_ref, *outs):
    channels = mixer_ref.shape[0] * mixer_ref.shape[1]
    mixer = mixer_ref[...].astype(jnp.float32).reshape(channels, mixer_ref.shape[2])
    mixer = mixer.T.astype(jnp.bfloat16)
    feats = outs[0].shape[1]
    for i, out in enumerate(outs):
        start = pl.multiple_of(target[i] * feats, feats)
        part = jnp.dot(mixer, w_ref[:, pl.ds(start, feats)], preferred_element_type=jnp.float32)
        out[...] = part.astype(out.dtype)


def layer(tokens, w_in, short_taps, skip_gain, filters, w_out):
    rows, feats = tokens.shape
    width, kinds, chan_dev = w_in.shape
    nx, ny = lax.axis_size("x"), lax.axis_size("yh")
    n_seq = lax.axis_size(SEQ)
    ix, iy = lax.axis_index("x"), lax.axis_index("yh")
    per = chan_dev // n_seq
    w3 = jnp.transpose(w_in, (1, 0, 2))
    shape, bf, f32 = jax.ShapeDtypeStruct, jnp.bfloat16, jnp.float32

    def x_of(d):
        return (ix + d + nx) % nx

    own = lax.axis_index(SEQ) * per
    group = chan_dev // filters.shape[0]
    lags, short, gain = call(
        prepare_body,
        [
            shape((n_seq * rows, rows), bf),
            shape((short_taps.shape[0], kinds, per, rows), f32),
            shape((per, rows), f32),
        ],
        [jnp.stack([own, own // group]), filters, short_taps, skip_gain[None]],
        "s",
        flops=8 * n_seq * rows * rows,
        nbytes=4 * n_seq * rows * rows,
    )

    steps = list(range(2, nx - 1)) + [1, nx - 1]
    across = chan_shift(tokens, 0, 1)
    near, far = [], []
    for d in steps:
        near.append(chan_shift(tokens, d, 0))
    for d in steps:
        far.append(chan_shift(across, d, 0))
    at_first = jnp.stack([ix * ny + iy, ix * ny + 1 - iy])
    at_near = jnp.stack([x_of(-d) * ny + iy for d in steps])
    at_far = jnp.stack([x_of(-d) * ny + 1 - iy for d in steps])
    work = dict(flops=2 * rows * width * kinds * chan_dev // 3, nbytes=width * kinds * chan_dev)
    partial = shape((kinds, rows, chan_dev), f32)
    order = jnp.concatenate([at_first, at_near, at_far])
    chunk = (kinds, feats, chan_dev)
    waits = pltpu.SemaphoreType.DMA((len(steps),))
    acc, w_next = call(
        project_first_body,
        [partial, shape((len(steps),) + chunk, bf)],
        [order, w3, tokens, across],
        "sh",
        scratch=[pltpu.VMEM((2,) + chunk, bf), pltpu.SemaphoreType.DMA((2,)), waits],
        vmem=46,
        **work,
    )
    acc, w_next = call(
        functools.partial(project_near_body, 2 + len(steps)),
        [partial, shape((len(steps),) + chunk, bf)],
        [order, w3, w_next] + near + [acc],
        "sh",
        scratch=[waits],
        vmem=46,
        **work,
    )
    proj = call(
        project_far_body, shape((n_seq, kinds, per, rows), bf), [w_next] + far + [acc], "", **work
    )
    proj = lax.all_to_all(proj, SEQ, 0, 0, tiled=True)
    mixer = call(
        mix_body,
        shape((n_seq, per, rows), bf),
        [proj, short, gain, lags],
        "",
        scratch=[pltpu.VMEM((n_seq * per, rows), f32)],
        flops=n_seq * per * n_seq * rows * rows,
        nbytes=4 * n_seq * rows * rows,
    )
    mixer = lax.all_to_all(mixer, SEQ, 0, 0, tiled=True)
    work = dict(flops=rows * chan_dev * width, nbytes=chan_dev * width)
    block, wide = shape((rows, feats), bf), shape((rows, feats), f32)
    to_near = jnp.stack([x_of(d) * ny + iy for d in steps + [0]])
    to_far = jnp.stack([x_of(d) * ny + 1 - iy for d in steps + [0]])
    sends = call(output_body, [block] * (nx - 1) + [wide], [to_far, mixer, w_out], "s", **work)
    partner = sends[-1]
    for d, part in zip(steps, sends):
        partner = partner + chan_shift(part, d, 0).astype(f32)
    partner = chan_shift(partner.astype(bf), 0, 1)
    sends = call(output_body, [block] * (nx - 1) + [wide], [to_near, mixer, w_out], "s", **work)
    total = sends[-1]
    for d, part in zip(steps, sends):
        total = total + chan_shift(part, d, 0).astype(f32)
    return (total + partner.astype(f32)).astype(bf)


def solution(mesh):
    fine = Mesh(mesh.devices.reshape(SPLIT), SEQ + CHAN)
    placed = (
        P(SEQ, CHAN),
        P(None, None, CHAN),
        P(None, None, CHAN),
        P(CHAN),
        P(CHAN, None),
        P(CHAN, None),
    )
    return jax.shard_map(layer, mesh=fine, in_specs=placed, out_specs=P(SEQ, CHAN), check_vma=False)
```

profile of v0, /device:TPU:2, one launch (start us, length us, event | category | flops | bytes accessed | tf_op | source)
XLA Modules:
  0.0 74.8 jit_solution(13273436387131262155)
XLA Ops:
  0.0 3.2 %collective-permute-start = (bf16[128,512]{1,0:T(8,128)(2,1)}, bf16[128,512]{1,0:T(8,128)(2,1)S(1)}, u32[]{:S(2)}, u32[]{:S(2)}) collective-permute-start(bf16[128,512]{1,0:T(8,128)(2,1)} %refs_0_.1), channel_id=1, source_target_pairs={{0,1},{1,0},{2,3},{3,2},{4,5},{5,4},{6,7},{7,6},{8,9},{9,8},{10,11... | collective-permute-start | bytes 393224 | tf_op jit(solution)/shard_map/ppermute | solution.py:25
  3.2 2.1 %collective-permute-start.1 = (bf16[128,512]{1,0:T(8,128)(2,1)}, bf16[128,512]{1,0:T(8,128)(2,1)S(1)}, u32[]{:S(2)}, u32[]{:S(2)}) collective-permute-start(bf16[128,512]{1,0:T(8,128)(2,1)} %refs_0_.1), channel_id=1, source_target_pairs={{0,4},{1,5},{2,6},{3,7},{4,0},{5,1},{6,2},{7,3},{8,12},{9,13},{10,... | collective-permute-start | bytes 393224 | tf_op jit(solution)/shard_map/ppermute | solution.py:25
  5.3 2.0 %collective-permute-start.3 = (bf16[128,512]{1,0:T(8,128)(2,1)}, bf16[128,512]{1,0:T(8,128)(2,1)S(1)}, u32[]{:S(2)}, u32[]{:S(2)}) collective-permute-start(bf16[128,512]{1,0:T(8,128)(2,1)} %refs_0_.1), channel_id=1, source_target_pairs={{0,6},{1,7},{2,0},{3,1},{4,2},{5,3},{6,4},{7,5},{8,14},{9,15},{10,... | collective-permute-start | bytes 393224 | tf_op jit(solution)/shard_map/ppermute | solution.py:25
  7.4 1.7 %collective-permute-start.4 = (bf16[128,512]{1,0:T(8,128)(2,1)S(1)}, bf16[128,512]{1,0:T(8,128)(2,1)S(1)}, u32[]{:S(2)}, u32[]{:S(2)}) collective-permute-start(bf16[128,512]{1,0:T(8,128)(2,1)S(1)} %collective-permute-done.refs_1_), channel_id=1, source_target_pairs={{0,4},{1,5},{2,6},{3,7},{4,0},{5,1},{6,2},{7,3},{8,12},{9,13},{10,... | collective-permute-start | bytes 393224 | tf_op jit(solution)/shard_map/ppermute | solution.py:25
  9.1 2.4 %collective-permute-start.5 = (bf16[128,512]{1,0:T(8,128)(2,1)S(1)}, bf16[128,512]{1,0:T(8,128)(2,1)S(1)}, u32[]{:S(2)}, u32[]{:S(2)}) collective-permute-start(bf16[128,512]{1,0:T(8,128)(2,1)S(1)} %collective-permute-done.refs_1_), channel_id=1, source_target_pairs={{0,2},{1,3},{2,4},{3,5},{4,6},{5,7},{6,0},{7,1},{8,10},{9,11},{10,... | collective-permute-start | bytes 393224 | tf_op jit(solution)/shard_map/ppermute | solution.py:25
  11.6 0.9 %copy-done.2 = bf16[128,512]{1,0:T(8,128)(2,1)S(1)} copy-done((bf16[128,512]{1,0:T(8,128)(2,1)S(1)}, bf16[128,512]{1,0:T(8,128)(2,1)}, u32[]{:S(2)}) %copy-start.2) | copy-done | bytes 131096
  12.5 2.7 %shard_map.64 = (f32[3,128,256]{2,1,0:T(8,128)S(1)}, bf16[3,3,512,256]{3,2,1,0:T(8,128)(2,1)S(1)}) custom-call(s32[8]{0:T(128)S(1)} %concatenate.3.order, bf16[3,4096,256]{2,1,0:T(8,128)(2,1)} %bitcast.21, bf16[128,512]{1,0:T(8,128)(2,1)S(1)} %copy-done.2, bf16[128,512]{1,0:T(8,128)(2,1)S(1)} %collective-permute-done.refs_1_), custom_call_target="tpu_custom_call" | custom-call | flops 268435456 | bytes 3145728 | tf_op jit(solution)/shard_map/pallas_call | solution.py:30
  15.2 2.5 %shard_map.65 = (f32[3,128,256]{2,1,0:T(8,128)S(1)}, bf16[3,3,512,256]{3,2,1,0:T(8,128)(2,1)S(1)}) custom-call(s32[8]{0:T(128)S(1)} %concatenate.3.order, bf16[3,4096,256]{2,1,0:T(8,128)(2,1)} %bitcast.22, bf16[3,3,512,256]{3,2,1,0:T(8,128)(2,1)S(1)} %get-tuple-element.20.w_ref, bf16[128,512]{1,0:T(8,128)(2,1)S(1)} %collective-permute-done.1.refs_0_, ...), custom_call_target="tpu_custom_call" | custom-call | flops 268435456 | bytes 3145728 | tf_op jit(solution)/shard_map/pallas_call | solution.py:30
  18.4 1.2 %shard_map.66 = bf16[32,3,8,128]{3,2,1,0:T(8,128)(2,1)} custom-call(bf16[3,3,512,256]{3,2,1,0:T(8,128)(2,1)S(1)} %get-tuple-element.22.w_ref, bf16[128,512]{1,0:T(8,128)(2,1)S(1)} %collective-permute-done.4.refs_0_, bf16[128,512]{1,0:T(8,128)(2,1)S(1)} %collective-permute-done.5.refs_1_, bf16[128,512]{1,0:T(8,128)(2,1)S(1)} %collective-permute-done.6.refs_2_, ...), custom_call_target="tpu_custom_call" | custom-call | flops 268435456 | bytes 3145728 | tf_op jit(solution)/shard_map/pallas_call | solution.py:30
  19.6 9.0 %all-to-all-start = ((bf16[32,3,8,128]{3,2,1,0:T(8,128)(2,1)}), bf16[32,3,8,128]{3,2,1,0:T(8,128)(2,1)S(1)}, u32[]{:S(2)}, u32[]{:S(2)}) async-start(bf16[32,3,8,128]{3,2,1,0:T(8,128)(2,1)} %shard_map.66), calls=%async_computation | async-start | bytes 393216 | tf_op jit(solution)/shard_map/all_to_all | solution.py:222
  28.7 0.9 %copy-done.1 = f32[16,4096]{1,0:T(8,128)S(1)} copy-done((f32[16,4096]{1,0:T(8,128)S(1)}, f32[16,4096]{1,0:T(8,128)}, u32[]{:S(2)}) %copy-start.1) | copy-done | bytes 262168
  29.6 0.9 %shard_map.67 = (bf16[4096,128]{1,0:T(8,128)(2,1)S(1)}, f32[3,3,8,128]{3,2,1,0:T(8,128)S(1)}, f32[8,128]{1,0:T(8,128)S(1)}) custom-call(s32[2]{0:T(128)S(1)} %pad_add_fusion.1.own_ref, f32[16,4096]{1,0:T(8,128)S(1)} %copy-done.1, f32[3,3,256]{2,1,0:T(4,128)S(1)} %copy-done.3, f32[1,256]{1,0:T(1,128)S(1)} %bitcast.20), custom_call_target="tpu_custom_call" | custom-call | flops 4194304 | bytes 2097152 | tf_op jit(solution)/shard_map/pallas_call | solution.py:30
  30.6 9.8 %all-to-all-done.proj_ref = bf16[32,3,8,128]{3,2,1,0:T(8,128)(2,1)S(1)} async-done(((bf16[32,3,8,128]{3,2,1,0:T(8,128)(2,1)}), bf16[32,3,8,128]{3,2,1,0:T(8,128)(2,1)S(1)}, u32[]{:S(2)}, u32[]{:S(2)}) %all-to-all-start) | async-done | bytes 196640 | tf_op jit(solution)/shard_map/all_to_all | solution.py:222
  40.4 1.2 %shard_map.68 = bf16[32,8,128]{2,1,0:T(8,128)(2,1)} custom-call(bf16[32,3,8,128]{3,2,1,0:T(8,128)(2,1)S(1)} %all-to-all-done.proj_ref, f32[3,3,8,128]{3,2,1,0:T(8,128)S(1)} %get-tuple-element.24.short_ref, f32[8,128]{1,0:T(8,128)S(1)} %get-tuple-element.25.gain_ref, bf16[4096,128]{1,0:T(8,128)(2,1)S(1)} %get-tuple-element.26.lags_ref), custom_call_target="tpu_custom_call" | custom-call | flops 134217728 | bytes 2097152 | tf_op jit(solution)/shard_map/pallas_call | solution.py:30
  41.5 3.9 %all-to-all-start.1 = ((bf16[32,8,128]{2,1,0:T(8,128)(2,1)}), bf16[32,8,128]{2,1,0:T(8,128)(2,1)S(1)}, u32[]{:S(2)}, u32[]{:S(2)}) async-start(bf16[32,8,128]{2,1,0:T(8,128)(2,1)} %shard_map.68), calls=%async_computation.1 | async-start | bytes 131072 | tf_op jit(solution)/shard_map/all_to_all | solution.py:232
  45.5 8.9 %all-to-all-done.1.mixer_ref = bf16[32,8,128]{2,1,0:T(8,128)(2,1)S(1)} async-done(((bf16[32,8,128]{2,1,0:T(8,128)(2,1)}), bf16[32,8,128]{2,1,0:T(8,128)(2,1)S(1)}, u32[]{:S(2)}, u32[]{:S(2)}) %all-to-all-start.1) | async-done | bytes 65568 | tf_op jit(solution)/shard_map/all_to_all | solution.py:232
  54.4 0.9 %shard_map.70 = (bf16[128,512]{1,0:T(8,128)(2,1)S(1)}, bf16[128,512]{1,0:T(8,128)(2,1)S(1)}, bf16[128,512]{1,0:T(8,128)(2,1)S(1)}, f32[128,512]{1,0:T(8,128)S(1)}) custom-call(s32[4]{0:T(128)S(1)} %pad_add_fusion.2.target, bf16[32,8,128]{2,1,0:T(8,128)(2,1)S(1)} %all-to-all-done.1.mixer_ref, bf16[256,4096]{1,0:T(8,128)(2,1)S(1)} %copy-done), custom_call_target="tpu_custom_call" | custom-call | flops 134217728 | bytes 1048576 | tf_op jit(solution)/shard_map/pallas_call | solution.py:30
  55.3 3.4 %collective-permute-start.10 = (bf16[128,512]{1,0:T(8,128)(2,1)S(1)}, bf16[128,512]{1,0:T(8,128)(2,1)S(1)}, u32[]{:S(2)}, u32[]{:S(2)}) collective-permute-start(bf16[128,512]{1,0:T(8,128)(2,1)S(1)} %get-tuple-element.32), channel_id=1, source_target_pairs={{0,4},{1,5},{2,6},{3,7},{4,0},{5,1},{6,2},{7,3},{8,12},{9,13},{10,... | collective-permute-start | bytes 393224 | tf_op jit(solution)/shard_map/ppermute | solution.py:25
  59.5 1.3 %collective-permute-start.12 = (bf16[128,512]{1,0:T(8,128)(2,1)S(1)}, bf16[128,512]{1,0:T(8,128)(2,1)S(1)}, u32[]{:S(2)}, u32[]{:S(2)}) collective-permute-start(bf16[128,512]{1,0:T(8,128)(2,1)S(1)} %get-tuple-element.34), channel_id=1, source_target_pairs={{0,6},{1,7},{2,0},{3,1},{4,2},{5,3},{6,4},{7,5},{8,14},{9,15},{10,... | collective-permute-start | bytes 393224 | tf_op jit(solution)/shard_map/ppermute | solution.py:25
  60.8 0.9 %shard_map.69 = (bf16[128,512]{1,0:T(8,128)(2,1)S(1)}, bf16[128,512]{1,0:T(8,128)(2,1)S(1)}, bf16[128,512]{1,0:T(8,128)(2,1)S(1)}, f32[128,512]{1,0:T(8,128)S(1)}) custom-call(s32[4]{0:T(128)S(1)} %pad_add_fusion.target, bf16[32,8,128]{2,1,0:T(8,128)(2,1)S(1)} %all-to-all-done.1.mixer_ref, bf16[256,4096]{1,0:T(8,128)(2,1)S(1)} %copy-done), custom_call_target="tpu_custom_call" | custom-call | flops 134217728 | bytes 1048576 | tf_op jit(solution)/shard_map/pallas_call | solution.py:30
  62.1 2.6 %collective-permute-start.8 = (bf16[128,512]{1,0:T(8,128)(2,1)S(1)}, bf16[128,512]{1,0:T(8,128)(2,1)S(1)}, u32[]{:S(2)}, u32[]{:S(2)}) collective-permute-start(bf16[128,512]{1,0:T(8,128)(2,1)S(1)} %get-tuple-element.29), channel_id=1, source_target_pairs={{0,2},{1,3},{2,4},{3,5},{4,6},{5,7},{6,0},{7,1},{8,10},{9,11},{10,... | collective-permute-start | bytes 393224 | tf_op jit(solution)/shard_map/ppermute | solution.py:25
  64.7 0.9 %collective-permute-start.9 = (bf16[128,512]{1,0:T(8,128)(2,1)S(1)}, bf16[128,512]{1,0:T(8,128)(2,1)S(1)}, u32[]{:S(2)}, u32[]{:S(2)}) collective-permute-start(bf16[128,512]{1,0:T(8,128)(2,1)S(1)} %get-tuple-element.30), channel_id=1, source_target_pairs={{0,6},{1,7},{2,0},{3,1},{4,2},{5,3},{6,4},{7,5},{8,14},{9,15},{10,... | collective-permute-start | bytes 393224 | tf_op jit(solution)/shard_map/ppermute | solution.py:25
  66.3 4.8 %collective-permute-start.13 = (bf16[128,512]{1,0:T(8,128)(2,1)S(1)}, bf16[128,512]{1,0:T(8,128)(2,1)S(1)}, u32[]{:S(2)}, u32[]{:S(2)}) collective-permute-start(bf16[128,512]{1,0:T(8,128)(2,1)S(1)} %add_convert_fusion.1), channel_id=1, source_target_pairs={{0,1},{1,0},{2,3},{3,2},{4,5},{5,4},{6,7},{7,6},{8,9},{9,8},{10,11... | collective-permute-start | bytes 393224 | tf_op jit(solution)/shard_map/ppermute | solution.py:25
  71.1 2.9 %collective-permute-done.13 = bf16[128,512]{1,0:T(8,128)(2,1)S(1)} collective-permute-done((bf16[128,512]{1,0:T(8,128)(2,1)S(1)}, bf16[128,512]{1,0:T(8,128)(2,1)S(1)}, u32[]{:S(2)}, u32[]{:S(2)}) %collective-permute-start.13) | collective-permute-done | bytes 131104 | tf_op jit(solution)/shard_map/ppermute | solution.py:25
  (31 shorter events, 3.5 us)
Async XLA Ops:
  0.0 7.3 %collective-permute-start = (bf16[128,512]{1,0:T(8,128)(2,1)}, bf16[128,512]{1,0:T(8,128)(2,1)S(1)}, u32[]{:S(2)}, u32[]{:S(2)}) collective-permute-start(bf16[128,512]{1,0:T(8,128)(2,1)} %refs_0_.1), channel_id=1, source_target_pairs={{0,1},{1,0},{2,3},{3,2},{4,5},{5,4},{6,7},{7,6},{8,9},{9,8},{10,11... | collective-permute-start | bytes 393224 | tf_op jit(solution)/shard_map/ppermute | solution.py:25
  3.2 8.3 %collective-permute-start.1 = (bf16[128,512]{1,0:T(8,128)(2,1)}, bf16[128,512]{1,0:T(8,128)(2,1)S(1)}, u32[]{:S(2)}, u32[]{:S(2)}) collective-permute-start(bf16[128,512]{1,0:T(8,128)(2,1)} %refs_0_.1), channel_id=1, source_target_pairs={{0,4},{1,5},{2,6},{3,7},{4,0},{5,1},{6,2},{7,3},{8,12},{9,13},{10,... | collective-permute-start | bytes 393224 | tf_op jit(solution)/shard_map/ppermute | solution.py:25
  5.3 9.9 %collective-permute-start.2 = (bf16[128,512]{1,0:T(8,128)(2,1)}, bf16[128,512]{1,0:T(8,128)(2,1)S(1)}, u32[]{:S(2)}, u32[]{:S(2)}) collective-permute-start(bf16[128,512]{1,0:T(8,128)(2,1)} %refs_0_.1), channel_id=1, source_target_pairs={{0,2},{1,3},{2,4},{3,5},{4,6},{5,7},{6,0},{7,1},{8,10},{9,11},{10,... | collective-permute-start | bytes 393224 | tf_op jit(solution)/shard_map/ppermute | solution.py:25
  5.3 9.9 %collective-permute-start.3 = (bf16[128,512]{1,0:T(8,128)(2,1)}, bf16[128,512]{1,0:T(8,128)(2,1)S(1)}, u32[]{:S(2)}, u32[]{:S(2)}) collective-permute-start(bf16[128,512]{1,0:T(8,128)(2,1)} %refs_0_.1), channel_id=1, source_target_pairs={{0,6},{1,7},{2,0},{3,1},{4,2},{5,3},{6,4},{7,5},{8,14},{9,15},{10,... | collective-permute-start | bytes 393224 | tf_op jit(solution)/shard_map/ppermute | solution.py:25
  7.4 10.4 %collective-permute-start.4 = (bf16[128,512]{1,0:T(8,128)(2,1)S(1)}, bf16[128,512]{1,0:T(8,128)(2,1)S(1)}, u32[]{:S(2)}, u32[]{:S(2)}) collective-permute-start(bf16[128,512]{1,0:T(8,128)(2,1)S(1)} %collective-permute-done.refs_1_), channel_id=1, source_target_pairs={{0,4},{1,5},{2,6},{3,7},{4,0},{5,1},{6,2},{7,3},{8,12},{9,13},{10,... | collective-permute-start | bytes 393224 | tf_op jit(solution)/shard_map/ppermute | solution.py:25
  9.1 9.3 %collective-permute-start.5 = (bf16[128,512]{1,0:T(8,128)(2,1)S(1)}, bf16[128,512]{1,0:T(8,128)(2,1)S(1)}, u32[]{:S(2)}, u32[]{:S(2)}) collective-permute-start(bf16[128,512]{1,0:T(8,128)(2,1)S(1)} %collective-permute-done.refs_1_), channel_id=1, source_target_pairs={{0,2},{1,3},{2,4},{3,5},{4,6},{5,7},{6,0},{7,1},{8,10},{9,11},{10,... | collective-permute-start | bytes 393224 | tf_op jit(solution)/shard_map/ppermute | solution.py:25
  11.5 6.9 %collective-permute-start.6 = (bf16[128,512]{1,0:T(8,128)(2,1)S(1)}, bf16[128,512]{1,0:T(8,128)(2,1)S(1)}, u32[]{:S(2)}, u32[]{:S(2)}) collective-permute-start(bf16[128,512]{1,0:T(8,128)(2,1)S(1)} %collective-permute-done.refs_1_), channel_id=1, source_target_pairs={{0,6},{1,7},{2,0},{3,1},{4,2},{5,3},{6,4},{7,5},{8,14},{9,15},{10,... | collective-permute-start | bytes 393224 | tf_op jit(solution)/shard_map/ppermute | solution.py:25
  11.6 0.9 %copy-start.2 = (bf16[128,512]{1,0:T(8,128)(2,1)S(1)}, bf16[128,512]{1,0:T(8,128)(2,1)}, u32[]{:S(2)}) copy-start(bf16[128,512]{1,0:T(8,128)(2,1)} %refs_0_.1) | copy-start | bytes 393220
  17.7 11.0 %copy-start.3 = (f32[3,3,256]{2,1,0:T(4,128)S(1)}, f32[3,3,256]{2,1,0:T(4,128)}, u32[]{:S(2)}) copy-start(f32[3,3,256]{2,1,0:T(4,128)} %taps_ref.1) | copy-start | bytes 27652
  17.7 10.9 %copy-start.4 = (f32[256]{0:T(256)S(1)}, f32[256]{0:T(256)}, u32[]{:S(2)}) copy-start(f32[256]{0:T(256)} %param.9) | copy-start | bytes 3076
  18.4 36.1 %copy-start = (bf16[256,4096]{1,0:T(8,128)(2,1)S(1)}, bf16[256,4096]{1,0:T(8,128)(2,1)}, u32[]{:S(2)}) copy-start(bf16[256,4096]{1,0:T(8,128)(2,1)} %w_ref.3) | copy-start | bytes 6291460
  19.6 20.8 %all-to-all-start = ((bf16[32,3,8,128]{3,2,1,0:T(8,128)(2,1)}), bf16[32,3,8,128]{3,2,1,0:T(8,128)(2,1)S(1)}, u32[]{:S(2)}, u32[]{:S(2)}) async-start(bf16[32,3,8,128]{3,2,1,0:T(8,128)(2,1)} %shard_map.66), calls=%async_computation | async-start | bytes 393216 | tf_op jit(solution)/shard_map/all_to_all | solution.py:222
  28.7 1.0 %copy-start.1 = (f32[16,4096]{1,0:T(8,128)S(1)}, f32[16,4096]{1,0:T(8,128)}, u32[]{:S(2)}) copy-start(f32[16,4096]{1,0:T(8,128)} %filters_ref.1) | copy-start | bytes 786436
  41.5 12.9 %all-to-all-start.1 = ((bf16[32,8,128]{2,1,0:T(8,128)(2,1)}), bf16[32,8,128]{2,1,0:T(8,128)(2,1)S(1)}, u32[]{:S(2)}, u32[]{:S(2)}) async-start(bf16[32,8,128]{2,1,0:T(8,128)(2,1)} %shard_map.68), calls=%async_computation.1 | async-start | bytes 131072 | tf_op jit(solution)/shard_map/all_to_all | solution.py:232
  55.3 9.4 %collective-permute-start.10 = (bf16[128,512]{1,0:T(8,128)(2,1)S(1)}, bf16[128,512]{1,0:T(8,128)(2,1)S(1)}, u32[]{:S(2)}, u32[]{:S(2)}) collective-permute-start(bf16[128,512]{1,0:T(8,128)(2,1)S(1)} %get-tuple-element.32), channel_id=1, source_target_pairs={{0,4},{1,5},{2,6},{3,7},{4,0},{5,1},{6,2},{7,3},{8,12},{9,13},{10,... | collective-permute-start | bytes 393224 | tf_op jit(solution)/shard_map/ppermute | solution.py:25
  58.7 6.9 %collective-permute-start.11 = (bf16[128,512]{1,0:T(8,128)(2,1)S(1)}, bf16[128,512]{1,0:T(8,128)(2,1)S(1)}, u32[]{:S(2)}, u32[]{:S(2)}) collective-permute-start(bf16[128,512]{1,0:T(8,128)(2,1)S(1)} %get-tuple-element.33), channel_id=1, source_target_pairs={{0,2},{1,3},{2,4},{3,5},{4,6},{5,7},{6,0},{7,1},{8,10},{9,11},{10,... | collective-permute-start | bytes 393224 | tf_op jit(solution)/shard_map/ppermute | solution.py:25
  59.5 6.8 %collective-permute-start.12 = (bf16[128,512]{1,0:T(8,128)(2,1)S(1)}, bf16[128,512]{1,0:T(8,128)(2,1)S(1)}, u32[]{:S(2)}, u32[]{:S(2)}) collective-permute-start(bf16[128,512]{1,0:T(8,128)(2,1)S(1)} %get-tuple-element.34), channel_id=1, source_target_pairs={{0,6},{1,7},{2,0},{3,1},{4,2},{5,3},{6,4},{7,5},{8,14},{9,15},{10,... | collective-permute-start | bytes 393224 | tf_op jit(solution)/shard_map/ppermute | solution.py:25
  61.7 9.4 %collective-permute-start.7 = (bf16[128,512]{1,0:T(8,128)(2,1)S(1)}, bf16[128,512]{1,0:T(8,128)(2,1)S(1)}, u32[]{:S(2)}, u32[]{:S(2)}) collective-permute-start(bf16[128,512]{1,0:T(8,128)(2,1)S(1)} %get-tuple-element.28), channel_id=1, source_target_pairs={{0,4},{1,5},{2,6},{3,7},{4,0},{5,1},{6,2},{7,3},{8,12},{9,13},{10,... | collective-permute-start | bytes 393224 | tf_op jit(solution)/shard_map/ppermute | solution.py:25
  62.1 9.0 %collective-permute-start.8 = (bf16[128,512]{1,0:T(8,128)(2,1)S(1)}, bf16[128,512]{1,0:T(8,128)(2,1)S(1)}, u32[]{:S(2)}, u32[]{:S(2)}) collective-permute-start(bf16[128,512]{1,0:T(8,128)(2,1)S(1)} %get-tuple-element.29), channel_id=1, source_target_pairs={{0,2},{1,3},{2,4},{3,5},{4,6},{5,7},{6,0},{7,1},{8,10},{9,11},{10,... | collective-permute-start | bytes 393224 | tf_op jit(solution)/shard_map/ppermute | solution.py:25
  64.7 6.4 %collective-permute-start.9 = (bf16[128,512]{1,0:T(8,128)(2,1)S(1)}, bf16[128,512]{1,0:T(8,128)(2,1)S(1)}, u32[]{:S(2)}, u32[]{:S(2)}) collective-permute-start(bf16[128,512]{1,0:T(8,128)(2,1)S(1)} %get-tuple-element.30), channel_id=1, source_target_pairs={{0,6},{1,7},{2,0},{3,1},{4,2},{5,3},{6,4},{7,5},{8,14},{9,15},{10,... | collective-permute-start | bytes 393224 | tf_op jit(solution)/shard_map/ppermute | solution.py:25
  66.3 7.7 %collective-permute-start.13 = (bf16[128,512]{1,0:T(8,128)(2,1)S(1)}, bf16[128,512]{1,0:T(8,128)(2,1)S(1)}, u32[]{:S(2)}, u32[]{:S(2)}) collective-permute-start(bf16[128,512]{1,0:T(8,128)(2,1)S(1)} %add_convert_fusion.1), channel_id=1, source_target_pairs={{0,1},{1,0},{2,3},{3,2},{4,5},{5,4},{6,7},{7,6},{8,9},{9,8},{10,11... | collective-permute-start | bytes 393224 | tf_op jit(solution)/shard_map/ppermute | solution.py:25
where the time goes:
time: 75.5 us; the launch traced here: 74.8 us
  starting transfers between devices  38.4 us (51%)
  waiting for transfers between devices  22.9 us (30%)
  Pallas kernels  10.3 us (14%)
  local copies, waits for them, and re-layouts  1.96 us (3%)
  other arithmetic  1.04 us (1%)
    ppermute x14, starting transfers between devices, chan_shift(): return lax.ppermute(block, CHAN, pairs)  25.6 us
    pallas_call x7, Pallas kernels, call(): pl.pallas_call(body, out_shape=out_shape, in_specs=[pl.BlockSpec(memory_s...  10.3 us
    all_to_all x1, waiting for transfers between devices, layer(): proj = lax.all_to_all(proj, SEQ, 0, 0, tiled=True)  9.79 us
    all_to_all x1, starting transfers between devices, layer(): proj = lax.all_to_all(proj, SEQ, 0, 0, tiled=True)  8.96 us
    all_to_all x1, waiting for transfers between devices, layer(): mixer = lax.all_to_all(mixer, SEQ, 0, 0, tiled=True)  8.91 us
    ppermute x14, waiting for transfers between devices, chan_shift(): return lax.ppermute(block, CHAN, pairs)  4.18 us
    all_to_all x1, starting transfers between devices, layer(): mixer = lax.all_to_all(mixer, SEQ, 0, 0, tiled=True)  3.85 us
    unnamed x10, local copies, waits for them, and re-layouts  1.88 us
  transfers between devices with their start and end apart: 16, of which 5 were waited for; matrix products, arithmetic and copies ran while one was open for 1% of the time, Pallas kernels for 9%

commit v1 on v0

--- a/solution.py
+++ b/solution.py
@@ -1,5 +1,3 @@
-import functools
-
 import jax
 import jax.numpy as jnp
 from jax import lax
@@ -38,8 +36,8 @@
     )(*args)
 
 
-def prepare_body(own_ref, filters_ref, taps_ref, gain_ref, lags_ref, short_ref, skip_ref):
-    own, group = own_ref[0], own_ref[1]
+def lags_body(group_ref, filters_ref, lags_ref):
+    group = group_ref[0]
     size = lags_ref.shape[1]
     count = lags_ref.shape[0] // size
     before = jnp.zeros((size, size), jnp.float32)
@@ -50,6 +48,10 @@
         turned = pltpu.roll(both, 0, 1, stride=1, stride_axis=0)
         lags_ref[k * size : (k + 1) * size, :] = turned[:, size:].astype(jnp.bfloat16)
         before = here
+
+
+def spread_body(own_ref, taps_ref, gain_ref, short_ref, skip_ref):
+    own, size = own_ref[0], skip_ref.shape[1]
     per, width = short_ref.shape[2], taps_ref.shape[2]
     lane = lax.broadcasted_iota(jnp.int32, (per, width), 1)
     row = lax.broadcasted_iota(jnp.int32, (per, width), 0)
@@ -66,16 +68,25 @@
 
 
 def fetch(order, skip, w_hbm, into, sem):
-    feats = into.shape[2]
     loads = []
     for i in range(into.shape[0]):
-        start = pl.multiple_of(order[skip + i] * feats, feats)
-        loads.append(pltpu.make_async_copy(w_hbm.at[:, pl.ds(start, feats)], into.at[i], sem.at[i]))
+        loads.append(pltpu.make_async_copy(w_hbm.at[:, order[skip + i]], into.at[i], sem.at[i]))
         loads[-1].start()
     return loads
 
 
-def project_first_body(order, w_hbm, *refs):
+def columns_body(other_ref, w_hbm, out_ref, sem):
+    parts, feats = out_ref.shape[0], out_ref.shape[2]
+    loads = []
+    for x in range(parts):
+        start = pl.multiple_of((2 * x + other_ref[0]) * feats, feats)
+        loads.append(pltpu.make_async_copy(w_hbm.at[:, pl.ds(start, feats)], out_ref.at[x], sem.at[x]))
+        loads[-1].start()
+    for load in loads:
+        load.wait()
+
+
+def project_near_body(order, w_hbm, *refs):
     blocks, (out_ref, next_ref, w_ref, sem, next_sem) = refs[:-5], refs[-5:]
     count = len(blocks)
     loads = fetch(order, 0, w_hbm, w_ref, sem)
@@ -85,18 +96,6 @@
         for k in range(w_ref.shape[1]):
             part = jnp.dot(block[...], w_ref[i, k], preferred_element_type=jnp.float32)
             out_ref[k] = part if i == 0 else out_ref[k] + part
-    for load in later:
-        load.wait()
-
-
-def project_near_body(skip, order, w_hbm, w_ref, *refs):
-    blocks, (before_ref, out_ref, next_ref, next_sem) = refs[:-4], refs[-4:]
-    later = fetch(order, skip, w_hbm, next_ref, next_sem)
-    for k in range(w_ref.shape[1]):
-        total = before_ref[k]
-        for i, block in enumerate(blocks):
-            total = total + jnp.dot(block[...], w_ref[i, k], preferred_element_type=jnp.float32)
-        out_ref[k] = total
     for load in later:
         load.wait()
 
@@ -140,19 +139,27 @@
             lags_ref[2 * size * m : 2 * size * (m + 1), :],
             preferred_element_type=jnp.float32,
         )
-    mixed = stream(0) * acc_ref[...]
-    out_ref[...] = mixed.reshape(count, width, size).astype(jnp.bfloat16)
-
-
-def output_body(target, mixer_ref, w_ref, *outs):
-    channels = mixer_ref.shape[0] * mixer_ref.shape[1]
-    mixer = mixer_ref[...].astype(jnp.float32).reshape(channels, mixer_ref.shape[2])
-    mixer = mixer.T.astype(jnp.bfloat16)
+    mixed = (stream(0) * acc_ref[...]).reshape(count, width, size).astype(jnp.bfloat16)
+    for y in range(out_ref.shape[1]):
+        out_ref[:, y] = mixed
+
+
+def output_body(index, mixer_ref, w_ref, other_ref, *outs):
+    iy = index[0]
+    count, ny, per, rows = mixer_ref.shape
     feats = outs[0].shape[1]
+
+    def mixer_of(y):
+        mixer = mixer_ref[:, y].astype(jnp.float32).reshape(count * per, rows)
+        return mixer.T.astype(jnp.bfloat16)
+
+    mine, others = mixer_of(iy), mixer_of(1 - iy)
     for i, out in enumerate(outs):
-        start = pl.multiple_of(target[i] * feats, feats)
-        part = jnp.dot(mixer, w_ref[:, pl.ds(start, feats)], preferred_element_type=jnp.float32)
-        out[...] = part.astype(out.dtype)
+        x = index[1 + i]
+        start = pl.multiple_of((ny * x + iy) * feats, feats)
+        total = jnp.dot(mine, w_ref[:, pl.ds(start, feats)], preferred_element_type=jnp.float32)
+        total = total + jnp.dot(others, other_ref[x], preferred_element_type=jnp.float32)
+        out[...] = total.astype(out.dtype)
 
 
 def layer(tokens, w_in, short_taps, skip_gain, filters, w_out):
@@ -162,7 +169,7 @@
     n_seq = lax.axis_size(SEQ)
     ix, iy = lax.axis_index("x"), lax.axis_index("yh")
     per = chan_dev // n_seq
-    w3 = jnp.transpose(w_in, (1, 0, 2))
+    w3 = jnp.transpose(w_in, (1, 0, 2)).reshape(kinds, nx * ny, feats, chan_dev)
     shape, bf, f32 = jax.ShapeDtypeStruct, jnp.bfloat16, jnp.float32
 
     def x_of(d):
@@ -170,14 +177,16 @@
 
     own = lax.axis_index(SEQ) * per
     group = chan_dev // filters.shape[0]
-    lags, short, gain = call(
-        prepare_body,
-        [
-            shape((n_seq * rows, rows), bf),
-            shape((short_taps.shape[0], kinds, per, rows), f32),
-            shape((per, rows), f32),
-        ],
-        [jnp.stack([own, own // group]), filters, short_taps, skip_gain[None]],
+    short, gain = call(
+        spread_body,
+        [shape((short_taps.shape[0], kinds, per, rows), f32), shape((per, rows), f32)],
+        [own[None], short_taps, skip_gain[None]],
+        "s",
+    )
+    lags = call(
+        lags_body,
+        shape((n_seq * rows, rows), bf),
+        [(own // group)[None], filters],
         "s",
         flops=8 * n_seq * rows * rows,
         nbytes=4 * n_seq * rows * rows,
@@ -197,53 +206,55 @@
     partial = shape((kinds, rows, chan_dev), f32)
     order = jnp.concatenate([at_first, at_near, at_far])
     chunk = (kinds, feats, chan_dev)
-    waits = pltpu.SemaphoreType.DMA((len(steps),))
+    first, dma = 2 + len(steps), pltpu.SemaphoreType.DMA
+    columns = call(
+        columns_body,
+        shape((nx, chan_dev, feats), bf),
+        [1 - iy[None], w_out],
+        "sh",
+        scratch=[dma((nx,))],
+        vmem=52,
+        nbytes=chan_dev * width,
+    )
     acc, w_next = call(
-        project_first_body,
+        project_near_body,
         [partial, shape((len(steps),) + chunk, bf)],
-        [order, w3, tokens, across],
+        [order, w3, tokens, across] + near,
         "sh",
-        scratch=[pltpu.VMEM((2,) + chunk, bf), pltpu.SemaphoreType.DMA((2,)), waits],
-        vmem=46,
-        **work,
-    )
-    acc, w_next = call(
-        functools.partial(project_near_body, 2 + len(steps)),
-        [partial, shape((len(steps),) + chunk, bf)],
-        [order, w3, w_next] + near + [acc],
-        "sh",
-        scratch=[waits],
-        vmem=46,
+        scratch=[pltpu.VMEM((first,) + chunk, bf), dma((first,)), dma((len(steps),))],
+        vmem=48,
         **work,
     )
     proj = call(
         project_far_body, shape((n_seq, kinds, per, rows), bf), [w_next] + far + [acc], "", **work
     )
+    columns = chan_shift(columns, 0, 1)
     proj = lax.all_to_all(proj, SEQ, 0, 0, tiled=True)
     mixer = call(
         mix_body,
-        shape((n_seq, per, rows), bf),
+        shape((n_seq, ny, per, rows), bf),
         [proj, short, gain, lags],
         "",
         scratch=[pltpu.VMEM((n_seq * per, rows), f32)],
         flops=n_seq * per * n_seq * rows * rows,
         nbytes=4 * n_seq * rows * rows,
     )
-    mixer = lax.all_to_all(mixer, SEQ, 0, 0, tiled=True)
-    work = dict(flops=rows * chan_dev * width, nbytes=chan_dev * width)
+    mixer = mixer.reshape(n_seq * ny, per, rows)
+    mixer = lax.all_to_all(mixer, SEQ + ("yh",), 0, 0, tiled=True)
+    mixer = mixer.reshape(n_seq, ny, per, rows)
     block, wide = shape((rows, feats), bf), shape((rows, feats), f32)
-    to_near = jnp.stack([x_of(d) * ny + iy for d in steps + [0]])
-    to_far = jnp.stack([x_of(d) * ny + 1 - iy for d in steps + [0]])
-    sends = call(output_body, [block] * (nx - 1) + [wide], [to_far, mixer, w_out], "s", **work)
-    partner = sends[-1]
-    for d, part in zip(steps, sends):
-        partner = partner + chan_shift(part, d, 0).astype(f32)
-    partner = chan_shift(partner.astype(bf), 0, 1)
-    sends = call(output_body, [block] * (nx - 1) + [wide], [to_near, mixer, w_out], "s", **work)
+    sends = call(
+        output_body,
+        [block] * (nx - 1) + [wide],
+        [jnp.stack([iy] + [x_of(d) for d in steps + [0]]), mixer, w_out, columns],
+        "s",
+        flops=2 * rows * chan_dev * width,
+        nbytes=2 * chan_dev * width,
+    )
     total = sends[-1]
     for d, part in zip(steps, sends):
         total = total + chan_shift(part, d, 0).astype(f32)
-    return (total + partner.astype(f32)).astype(bf)
+    return total.astype(bf)
 
 
 def solution(mesh):

time: 75.5 us -> 97.5 us (1.29)
  the two profiles are of different devices: /device:TPU:2 before, /device:TPU:1 now
where the time goes in v1:
time: 97.5 us; the launch traced here: 97.2 us
  waiting for transfers between devices  47.8 us (49%)
  starting transfers between devices  37.1 us (38%)
  Pallas kernels  10.3 us (11%)
  local copies, waits for them, and re-layouts  1.15 us (1%)
    ppermute x11, waiting for transfers between devices, chan_shift(): return lax.ppermute(block, CHAN, pairs)  28.3 us
    ppermute x11, starting transfers between devices, chan_shift(): return lax.ppermute(block, CHAN, pairs)  18.6 us
    all_to_all x1, starting transfers between devices, layer(): proj = lax.all_to_all(proj, SEQ, 0, 0, tiled=True)  11.7 us
    all_to_all x1, waiting for transfers between devices, layer(): mixer = lax.all_to_all(mixer, SEQ + ('yh',), 0, 0, tiled=True)  10.8 us
    pallas_call x7, Pallas kernels, call(): pl.pallas_call(body, out_shape=out_shape, in_specs=[pl.BlockSpec(memory_s...  10.3 us
    all_to_all x1, waiting for transfers between devices, layer(): proj = lax.all_to_all(proj, SEQ, 0, 0, tiled=True)  8.68 us
    all_to_all x1, starting transfers between devices, layer(): mixer = lax.all_to_all(mixer, SEQ + ('yh',), 0, 0, tiled=True)  6.79 us
  transfers between devices with their start and end apart: 13, of which 7 were waited for; matrix products, arithmetic and copies ran while one was open for 0% of the time, Pallas kernels for 7%

profile of v1, /device:TPU:1, one launch (start us, length us, event | category | flops | bytes accessed | tf_op | source)
XLA Modules:
  0.0 97.2 jit_solution(5533039264105210542)
XLA Ops:
  0.0 2.3 %shard_map.69 = bf16[4,256,512]{2,1,0:T(8,128)(2,1)} custom-call(s32[1]{0:T(128)S(6)} %sub.24.other_ref, bf16[256,4096]{1,0:T(8,128)(2,1)} %w_ref.1), custom_call_target="tpu_custom_call" | custom-call | flops 1 | bytes 1048576 | tf_op jit(solution)/shard_map/pallas_call | solution.py:28
  2.3 3.8 %collective-permute-start.7 = (bf16[4,256,512]{2,1,0:T(8,128)(2,1)}, bf16[4,256,512]{2,1,0:T(8,128)(2,1)}, u32[]{:S(2)}, u32[]{:S(2)}) collective-permute-start(bf16[4,256,512]{2,1,0:T(8,128)(2,1)} %shard_map.69), channel_id=1, source_target_pairs={{0,1},{1,0},{2,3},{3,2},{4,5},{5,4},{6,7},{7,6},{8,9},{9,8},{10,11... | collective-permute-start | bytes 3145736 | tf_op jit(solution)/shard_map/ppermute | solution.py:23
  6.2 2.7 %collective-permute-start.1 = (bf16[128,512]{1,0:T(8,128)(2,1)S(1)}, bf16[128,512]{1,0:T(8,128)(2,1)S(1)}, u32[]{:S(2)}, u32[]{:S(2)}) collective-permute-start(bf16[128,512]{1,0:T(8,128)(2,1)S(1)} %copy-done.2), channel_id=1, source_target_pairs={{0,4},{1,5},{2,6},{3,7},{4,0},{5,1},{6,2},{7,3},{8,12},{9,13},{10,... | collective-permute-start | bytes 393224 | tf_op jit(solution)/shard_map/ppermute | solution.py:23
  9.3 2.4 %collective-permute-start.3 = (bf16[128,512]{1,0:T(8,128)(2,1)S(1)}, bf16[128,512]{1,0:T(8,128)(2,1)S(1)}, u32[]{:S(2)}, u32[]{:S(2)}) collective-permute-start(bf16[128,512]{1,0:T(8,128)(2,1)S(1)} %copy-done.2), channel_id=1, source_target_pairs={{0,6},{1,7},{2,0},{3,1},{4,2},{5,3},{6,4},{7,5},{8,14},{9,15},{10,... | collective-permute-start | bytes 393224 | tf_op jit(solution)/shard_map/ppermute | solution.py:23
  11.6 19.3 %collective-permute-done.refs_1_ = bf16[128,512]{1,0:T(8,128)(2,1)S(1)} collective-permute-done((bf16[128,512]{1,0:T(8,128)(2,1)S(1)}, bf16[128,512]{1,0:T(8,128)(2,1)S(1)}, u32[]{:S(2)}, u32[]{:S(2)}) %collective-permute-start) | collective-permute-done | bytes 131104 | tf_op jit(solution)/shard_map/ppermute | solution.py:23
  31.0 3.5 %collective-permute-start.4 = (bf16[128,512]{1,0:T(8,128)(2,1)S(1)}, bf16[128,512]{1,0:T(8,128)(2,1)S(1)}, u32[]{:S(2)}, u32[]{:S(2)}) collective-permute-start(bf16[128,512]{1,0:T(8,128)(2,1)S(1)} %collective-permute-done.refs_1_), channel_id=1, source_target_pairs={{0,4},{1,5},{2,6},{3,7},{4,0},{5,1},{6,2},{7,3},{8,12},{9,13},{10,... | collective-permute-start | bytes 393224 | tf_op jit(solution)/shard_map/ppermute | solution.py:23
  34.8 2.4 %collective-permute-start.6 = (bf16[128,512]{1,0:T(8,128)(2,1)S(1)}, bf16[128,512]{1,0:T(8,128)(2,1)S(1)}, u32[]{:S(2)}, u32[]{:S(2)}) collective-permute-start(bf16[128,512]{1,0:T(8,128)(2,1)S(1)} %collective-permute-done.refs_1_), channel_id=1, source_target_pairs={{0,6},{1,7},{2,0},{3,1},{4,2},{5,3},{6,4},{7,5},{8,14},{9,15},{10,... | collective-permute-start | bytes 393224 | tf_op jit(solution)/shard_map/ppermute | solution.py:23
  37.3 3.5 %shard_map.64 = (f32[3,128,256]{2,1,0:T(8,128)S(1)}, bf16[3,3,512,256]{3,2,1,0:T(8,128)(2,1)S(1)}) custom-call(s32[8]{0:T(128)S(1)} %concatenate.3.order, bf16[3,8,512,256]{3,2,1,0:T(8,128)(2,1)} %bitcast.23, bf16[128,512]{1,0:T(8,128)(2,1)S(1)} %copy-done.2, bf16[128,512]{1,0:T(8,128)(2,1)S(1)} %collective-permute-done.refs_1_, ...), custom_call_target="tpu_custom_call" | custom-call | flops 268435456 | bytes 3145728 | tf_op jit(solution)/shard_map/pallas_call | solution.py:28
  40.8 0.5 collective-permute-done.5.refs_1_
  41.2 1.2 %shard_map.65 = bf16[32,3,8,128]{3,2,1,0:T(8,128)(2,1)} custom-call(bf16[3,3,512,256]{3,2,1,0:T(8,128)(2,1)S(1)} %get-tuple-element.13.w_ref, bf16[128,512]{1,0:T(8,128)(2,1)S(1)} %collective-permute-done.4.refs_0_, bf16[128,512]{1,0:T(8,128)(2,1)S(1)} %collective-permute-done.5.refs_1_, bf16[128,512]{1,0:T(8,128)(2,1)S(1)} %collective-permute-done.6.refs_2_, ...), custom_call_target="tpu_custom_call" | custom-call | flops 268435456 | bytes 3145728 | tf_op jit(solution)/shard_map/pallas_call | solution.py:28
  42.5 11.7 %all-to-all-start = ((bf16[32,3,8,128]{3,2,1,0:T(8,128)(2,1)}), bf16[32,3,8,128]{3,2,1,0:T(8,128)(2,1)S(1)}, u32[]{:S(2)}, u32[]{:S(2)}) async-start(bf16[32,3,8,128]{3,2,1,0:T(8,128)(2,1)} %shard_map.65), calls=%async_computation | async-start | bytes 393216 | tf_op jit(solution)/shard_map/all_to_all | solution.py:232
  54.3 1.0 copy-done.1
  55.3 0.4 shard_map.67.lags_ref
  55.6 8.7 %all-to-all-done.proj_ref = bf16[32,3,8,128]{3,2,1,0:T(8,128)(2,1)S(1)} async-done(((bf16[32,3,8,128]{3,2,1,0:T(8,128)(2,1)}), bf16[32,3,8,128]{3,2,1,0:T(8,128)(2,1)S(1)}, u32[]{:S(2)}, u32[]{:S(2)}) %all-to-all-start) | async-done | bytes 196640 | tf_op jit(solution)/shard_map/all_to_all | solution.py:232
  64.3 1.2 %shard_map.68 = bf16[32,2,8,128]{3,2,1,0:T(8,128)(2,1)} custom-call(bf16[32,3,8,128]{3,2,1,0:T(8,128)(2,1)S(1)} %all-to-all-done.proj_ref, f32[3,3,8,128]{3,2,1,0:T(8,128)S(1)} %get-tuple-element.15.short_ref, f32[8,128]{1,0:T(8,128)S(1)} %get-tuple-element.16.gain_ref, bf16[4096,128]{1,0:T(8,128)(2,1)S(1)} %shard_map.67.lags_ref), custom_call_target="tpu_custom_call" | custom-call | flops 134217728 | bytes 2097152 | tf_op jit(solution)/shard_map/pallas_call | solution.py:28
  65.5 6.8 %all-to-all-start.1 = ((bf16[64,8,128]{2,1,0:T(8,128)(2,1)}), bf16[64,8,128]{2,1,0:T(8,128)(2,1)S(1)}, u32[]{:S(2)}, u32[]{:S(2)}) async-start(bf16[64,8,128]{2,1,0:T(8,128)(2,1)} %bitcast.18), calls=%async_computation.1 | async-start | bytes 262144 | tf_op jit(solution)/shard_map/all_to_all | solution.py:243
  72.4 10.8 %all-to-all-done.1 = bf16[64,8,128]{2,1,0:T(8,128)(2,1)S(1)} async-done(((bf16[64,8,128]{2,1,0:T(8,128)(2,1)}), bf16[64,8,128]{2,1,0:T(8,128)(2,1)S(1)}, u32[]{:S(2)}, u32[]{:S(2)}) %all-to-all-start.1) | async-done | bytes 131104 | tf_op jit(solution)/shard_map/all_to_all | solution.py:243
  83.3 1.7 %shard_map.70 = (bf16[128,512]{1,0:T(8,128)(2,1)S(1)}, bf16[128,512]{1,0:T(8,128)(2,1)S(1)}, bf16[128,512]{1,0:T(8,128)(2,1)S(1)}, f32[128,512]{1,0:T(8,128)S(1)}) custom-call(s32[5]{0:T(128)S(1)} %stack.47.index, bf16[32,2,8,128]{3,2,1,0:T(8,128)(2,1)S(1)} %bitcast.21, bf16[256,4096]{1,0:T(8,128)(2,1)S(1)} %copy-done, ...), custom_call_target="tpu_custom_call" | custom-call | flops 268435456 | bytes 2097152 | tf_op jit(solution)/shard_map/pallas_call | solution.py:28
  85.0 2.3 %collective-permute-start.10 = (bf16[128,512]{1,0:T(8,128)(2,1)S(1)}, bf16[128,512]{1,0:T(8,128)(2,1)S(1)}, u32[]{:S(2)}, u32[]{:S(2)}) collective-permute-start(bf16[128,512]{1,0:T(8,128)(2,1)S(1)} %get-tuple-element.20), channel_id=1, source_target_pairs={{0,6},{1,7},{2,0},{3,1},{4,2},{5,3},{6,4},{7,5},{8,14},{9,15},{10,... | collective-permute-start | bytes 393224 | tf_op jit(solution)/shard_map/ppermute | solution.py:23
  87.3 0.7 collective-permute-start.9
  88.0 2.4 %collective-permute-done.10 = bf16[128,512]{1,0:T(8,128)(2,1)S(1)} collective-permute-done((bf16[128,512]{1,0:T(8,128)(2,1)S(1)}, bf16[128,512]{1,0:T(8,128)(2,1)S(1)}, u32[]{:S(2)}, u32[]{:S(2)}) %collective-permute-start.10) | collective-permute-done | bytes 131104 | tf_op jit(solution)/shard_map/ppermute | solution.py:23
  90.4 2.9 %collective-permute-done.8 = bf16[128,512]{1,0:T(8,128)(2,1)S(1)} collective-permute-done((bf16[128,512]{1,0:T(8,128)(2,1)S(1)}, bf16[128,512]{1,0:T(8,128)(2,1)S(1)}, u32[]{:S(2)}, u32[]{:S(2)}) %collective-permute-start.8) | collective-permute-done | bytes 131104 | tf_op jit(solution)/shard_map/ppermute | solution.py:23
  93.3 3.2 %collective-permute-done.9 = bf16[128,512]{1,0:T(8,128)(2,1)S(1)} collective-permute-done((bf16[128,512]{1,0:T(8,128)(2,1)S(1)}, bf16[128,512]{1,0:T(8,128)(2,1)S(1)}, u32[]{:S(2)}, u32[]{:S(2)}) %collective-permute-start.9) | collective-permute-done | bytes 131104 | tf_op jit(solution)/shard_map/ppermute | solution.py:23
  96.5 0.7 add_convert_fusion
  (22 shorter events, 1.0 us)
Async XLA Ops:
  0.0 6.1 %copy-start.2 = (bf16[128,512]{1,0:T(8,128)(2,1)S(1)}, bf16[128,512]{1,0:T(8,128)(2,1)}, u32[]{:S(2)}) copy-start(bf16[128,512]{1,0:T(8,128)(2,1)} %refs_0_.1) | copy-start | bytes 393220
  2.3 81.0 %collective-permute-start.7 = (bf16[4,256,512]{2,1,0:T(8,128)(2,1)}, bf16[4,256,512]{2,1,0:T(8,128)(2,1)}, u32[]{:S(2)}, u32[]{:S(2)}) collective-permute-start(bf16[4,256,512]{2,1,0:T(8,128)(2,1)} %shard_map.69), channel_id=1, source_target_pairs={{0,1},{1,0},{2,3},{3,2},{4,5},{5,4},{6,7},{7,6},{8,9},{9,8},{10,11... | collective-permute-start | bytes 3145736 | tf_op jit(solution)/shard_map/ppermute | solution.py:23
  6.1 24.9 %collective-permute-start = (bf16[128,512]{1,0:T(8,128)(2,1)S(1)}, bf16[128,512]{1,0:T(8,128)(2,1)S(1)}, u32[]{:S(2)}, u32[]{:S(2)}) collective-permute-start(bf16[128,512]{1,0:T(8,128)(2,1)S(1)} %copy-done.2), channel_id=1, source_target_pairs={{0,1},{1,0},{2,3},{3,2},{4,5},{5,4},{6,7},{7,6},{8,9},{9,8},{10,11... | collective-permute-start | bytes 393224 | tf_op jit(solution)/shard_map/ppermute | solution.py:23
  6.2 28.3 %collective-permute-start.1 = (bf16[128,512]{1,0:T(8,128)(2,1)S(1)}, bf16[128,512]{1,0:T(8,128)(2,1)S(1)}, u32[]{:S(2)}, u32[]{:S(2)}) collective-permute-start(bf16[128,512]{1,0:T(8,128)(2,1)S(1)} %copy-done.2), channel_id=1, source_target_pairs={{0,4},{1,5},{2,6},{3,7},{4,0},{5,1},{6,2},{7,3},{8,12},{9,13},{10,... | collective-permute-start | bytes 393224 | tf_op jit(solution)/shard_map/ppermute | solution.py:23
  8.9 25.9 %collective-permute-start.2 = (bf16[128,512]{1,0:T(8,128)(2,1)S(1)}, bf16[128,512]{1,0:T(8,128)(2,1)S(1)}, u32[]{:S(2)}, u32[]{:S(2)}) collective-permute-start(bf16[128,512]{1,0:T(8,128)(2,1)S(1)} %copy-done.2), channel_id=1, source_target_pairs={{0,2},{1,3},{2,4},{3,5},{4,6},{5,7},{6,0},{7,1},{8,10},{9,11},{10,... | collective-permute-start | bytes 393224 | tf_op jit(solution)/shard_map/ppermute | solution.py:23
  9.3 28.0 %collective-permute-start.3 = (bf16[128,512]{1,0:T(8,128)(2,1)S(1)}, bf16[128,512]{1,0:T(8,128)(2,1)S(1)}, u32[]{:S(2)}, u32[]{:S(2)}) collective-permute-start(bf16[128,512]{1,0:T(8,128)(2,1)S(1)} %copy-done.2), channel_id=1, source_target_pairs={{0,6},{1,7},{2,0},{3,1},{4,2},{5,3},{6,4},{7,5},{8,14},{9,15},{10,... | collective-permute-start | bytes 393224 | tf_op jit(solution)/shard_map/ppermute | solution.py:23
  31.0 9.8 %collective-permute-start.4 = (bf16[128,512]{1,0:T(8,128)(2,1)S(1)}, bf16[128,512]{1,0:T(8,128)(2,1)S(1)}, u32[]{:S(2)}, u32[]{:S(2)}) collective-permute-start(bf16[128,512]{1,0:T(8,128)(2,1)S(1)} %collective-permute-done.refs_1_), channel_id=1, source_target_pairs={{0,4},{1,5},{2,6},{3,7},{4,0},{5,1},{6,2},{7,3},{8,12},{9,13},{10,... | collective-permute-start | bytes 393224 | tf_op jit(solution)/shard_map/ppermute | solution.py:23
  34.5 6.8 %collective-permute-start.5 = (bf16[128,512]{1,0:T(8,128)(2,1)S(1)}, bf16[128,512]{1,0:T(8,128)(2,1)S(1)}, u32[]{:S(2)}, u32[]{:S(2)}) collective-permute-start(bf16[128,512]{1,0:T(8,128)(2,1)S(1)} %collective-permute-done.refs_1_), channel_id=1, source_target_pairs={{0,2},{1,3},{2,4},{3,5},{4,6},{5,7},{6,0},{7,1},{8,10},{9,11},{10,... | collective-permute-start | bytes 393224 | tf_op jit(solution)/shard_map/ppermute | solution.py:23
  34.8 6.4 %collective-permute-start.6 = (bf16[128,512]{1,0:T(8,128)(2,1)S(1)}, bf16[128,512]{1,0:T(8,128)(2,1)S(1)}, u32[]{:S(2)}, u32[]{:S(2)}) collective-permute-start(bf16[128,512]{1,0:T(8,128)(2,1)S(1)} %collective-permute-done.refs_1_), channel_id=1, source_target_pairs={{0,6},{1,7},{2,0},{3,1},{4,2},{5,3},{6,4},{7,5},{8,14},{9,15},{10,... | collective-permute-start | bytes 393224 | tf_op jit(solution)/shard_map/ppermute | solution.py:23
  40.8 13.4 %copy-start.3 = (f32[3,3,256]{2,1,0:T(4,128)S(1)}, f32[3,3,256]{2,1,0:T(4,128)}, u32[]{:S(2)}) copy-start(f32[3,3,256]{2,1,0:T(4,128)} %taps_ref.1) | copy-start | bytes 27652
  40.8 13.4 %copy-start.4 = (f32[256]{0:T(256)S(1)}, f32[256]{0:T(256)}, u32[]{:S(2)}) copy-start(f32[256]{0:T(256)} %param.9) | copy-start | bytes 3076
  42.5 40.8 %copy-start = (bf16[256,4096]{1,0:T(8,128)(2,1)S(1)}, bf16[256,4096]{1,0:T(8,128)(2,1)}, u32[]{:S(2)}) copy-start(bf16[256,4096]{1,0:T(8,128)(2,1)} %w_ref.1) | copy-start | bytes 6291460
  42.5 21.8 %all-to-all-start = ((bf16[32,3,8,128]{3,2,1,0:T(8,128)(2,1)}), bf16[32,3,8,128]{3,2,1,0:T(8,128)(2,1)S(1)}, u32[]{:S(2)}, u32[]{:S(2)}) async-start(bf16[32,3,8,128]{3,2,1,0:T(8,128)(2,1)} %shard_map.65), calls=%async_computation | async-start | bytes 393216 | tf_op jit(solution)/shard_map/all_to_all | solution.py:232
  54.3 1.0 copy-start.1
  65.5 17.8 %all-to-all-start.1 = ((bf16[64,8,128]{2,1,0:T(8,128)(2,1)}), bf16[64,8,128]{2,1,0:T(8,128)(2,1)S(1)}, u32[]{:S(2)}, u32[]{:S(2)}) async-start(bf16[64,8,128]{2,1,0:T(8,128)(2,1)} %bitcast.18), calls=%async_computation.1 | async-start | bytes 262144 | tf_op jit(solution)/shard_map/all_to_all | solution.py:243
  85.0 5.4 %collective-permute-start.10 = (bf16[128,512]{1,0:T(8,128)(2,1)S(1)}, bf16[128,512]{1,0:T(8,128)(2,1)S(1)}, u32[]{:S(2)}, u32[]{:S(2)}) collective-permute-start(bf16[128,512]{1,0:T(8,128)(2,1)S(1)} %get-tuple-element.20), channel_id=1, source_target_pairs={{0,6},{1,7},{2,0},{3,1},{4,2},{5,3},{6,4},{7,5},{8,14},{9,15},{10,... | collective-permute-start | bytes 393224 | tf_op jit(solution)/shard_map/ppermute | solution.py:23
  87.3 6.0 %collective-permute-start.8 = (bf16[128,512]{1,0:T(8,128)(2,1)S(1)}, bf16[128,512]{1,0:T(8,128)(2,1)S(1)}, u32[]{:S(2)}, u32[]{:S(2)}) collective-permute-start(bf16[128,512]{1,0:T(8,128)(2,1)S(1)} %get-tuple-element.18), channel_id=1, source_target_pairs={{0,4},{1,5},{2,6},{3,7},{4,0},{5,1},{6,2},{7,3},{8,12},{9,13},{10,... | collective-permute-start | bytes 393224 | tf_op jit(solution)/shard_map/ppermute | solution.py:23
  87.3 9.1 %collective-permute-start.9 = (bf16[128,512]{1,0:T(8,128)(2,1)S(1)}, bf16[128,512]{1,0:T(8,128)(2,1)S(1)}, u32[]{:S(2)}, u32[]{:S(2)}) collective-permute-start(bf16[128,512]{1,0:T(8,128)(2,1)S(1)} %get-tuple-element.19), channel_id=1, source_target_pairs={{0,2},{1,3},{2,4},{3,5},{4,6},{5,7},{6,0},{7,1},{8,10},{9,11},{10,... | collective-permute-start | bytes 393224 | tf_op jit(solution)/shard_map/ppermute | solution.py:23

commit v2 on v1

--- a/solution.py
+++ b/solution.py
@@ -75,12 +75,12 @@
     return loads
 
 
-def columns_body(other_ref, w_hbm, out_ref, sem):
-    parts, feats = out_ref.shape[0], out_ref.shape[2]
-    loads = []
+def columns_body(index, w_hbm, out_ref, sem):
+    parts, half, feats = out_ref.shape
+    rows, loads = pl.ds(pl.multiple_of(index[1] * half, half), half), []
     for x in range(parts):
-        start = pl.multiple_of((2 * x + other_ref[0]) * feats, feats)
-        loads.append(pltpu.make_async_copy(w_hbm.at[:, pl.ds(start, feats)], out_ref.at[x], sem.at[x]))
+        start = pl.multiple_of((2 * x + index[0]) * feats, feats)
+        loads.append(pltpu.make_async_copy(w_hbm.at[rows, pl.ds(start, feats)], out_ref.at[x], sem.at[x]))
         loads[-1].start()
     for load in loads:
         load.wait()
@@ -144,21 +144,24 @@
         out_ref[:, y] = mixed
 
 
-def output_body(index, mixer_ref, w_ref, other_ref, *outs):
-    iy = index[0]
+def output_body(index, mixer_ref, w_ref, half_ref, twin_ref, *outs):
+    iy, core = index[0], index[1]
     count, ny, per, rows = mixer_ref.shape
-    feats = outs[0].shape[1]
-
-    def mixer_of(y):
-        mixer = mixer_ref[:, y].astype(jnp.float32).reshape(count * per, rows)
-        return mixer.T.astype(jnp.bfloat16)
-
-    mine, others = mixer_of(iy), mixer_of(1 - iy)
+    half, feats = count // 2, outs[0].shape[1]
+
+    def mixer_of(block):
+        block = block.astype(jnp.float32)
+        return block.reshape(block.shape[0] * per, rows).T.astype(jnp.bfloat16)
+
+    mine = mixer_of(mixer_ref[:, iy])
+    here = mixer_of(mixer_ref[pl.ds(core * half, half), 1 - iy])
+    there = mixer_of(mixer_ref[pl.ds((1 - core) * half, half), 1 - iy])
     for i, out in enumerate(outs):
-        x = index[1 + i]
+        x = index[2 + i]
         start = pl.multiple_of((ny * x + iy) * feats, feats)
         total = jnp.dot(mine, w_ref[:, pl.ds(start, feats)], preferred_element_type=jnp.float32)
-        total = total + jnp.dot(others, other_ref[x], preferred_element_type=jnp.float32)
+        total = total + jnp.dot(here, half_ref[x], preferred_element_type=jnp.float32)
+        total = total + jnp.dot(there, twin_ref[x], preferred_element_type=jnp.float32)
         out[...] = total.astype(out.dtype)
 
 
@@ -167,7 +170,7 @@
     width, kinds, chan_dev = w_in.shape
     nx, ny = lax.axis_size("x"), lax.axis_size("yh")
     n_seq = lax.axis_size(SEQ)
-    ix, iy = lax.axis_index("x"), lax.axis_index("yh")
+    ix, iy, core = lax.axis_index("x"), lax.axis_index("yh"), lax.axis_index("core")
     per = chan_dev // n_seq
     w3 = jnp.transpose(w_in, (1, 0, 2)).reshape(kinds, nx * ny, feats, chan_dev)
     shape, bf, f32 = jax.ShapeDtypeStruct, jnp.bfloat16, jnp.float32
@@ -198,7 +201,7 @@
     for d in steps:
         near.append(chan_shift(tokens, d, 0))
     for d in steps:
-        far.append(chan_shift(across, d, 0))
+        far.append(chan_shift(near[0], 0, 1) if d == 2 else chan_shift(across, d, 0))
     at_first = jnp.stack([ix * ny + iy, ix * ny + 1 - iy])
     at_near = jnp.stack([x_of(-d) * ny + iy for d in steps])
     at_far = jnp.stack([x_of(-d) * ny + 1 - iy for d in steps])
@@ -209,8 +212,8 @@
     first, dma = 2 + len(steps), pltpu.SemaphoreType.DMA
     columns = call(
         columns_body,
-        shape((nx, chan_dev, feats), bf),
-        [1 - iy[None], w_out],
+        shape((nx, chan_dev // 2, feats), bf),
+        [jnp.stack([1 - iy, core]), w_out],
         "sh",
         scratch=[dma((nx,))],
         vmem=52,
@@ -229,6 +232,7 @@
         project_far_body, shape((n_seq, kinds, per, rows), bf), [w_next] + far + [acc], "", **work
     )
     columns = chan_shift(columns, 0, 1)
+    twin = lax.ppermute(columns, "core", [(0, 1), (1, 0)])
     proj = lax.all_to_all(proj, SEQ, 0, 0, tiled=True)
     mixer = call(
         mix_body,
@@ -246,7 +250,7 @@
     sends = call(
         output_body,
         [block] * (nx - 1) + [wide],
-        [jnp.stack([iy] + [x_of(d) for d in steps + [0]]), mixer, w_out, columns],
+        [jnp.stack([iy, core] + [x_of(d) for d in steps + [0]]), mixer, w_out, columns, twin],
         "s",
         flops=2 * rows * chan_dev * width,
         nbytes=2 * chan_dev * width,

time: 97.5 us -> 82.7 us (0.85)
  the two profiles are of different devices: /device:TPU:1 before, /device:TPU:2 now
where the time goes in v2:
time: 82.7 us; the launch traced here: 81.6 us
  waiting for transfers between devices  37.1 us (45%)
  starting transfers between devices  32.5 us (39%)
  Pallas kernels  9.88 us (12%)
  local copies, waits for them, and re-layouts  1.15 us (1%)
    ppermute x11, starting transfers between devices, chan_shift(): return lax.ppermute(block, CHAN, pairs)  17.2 us
    ppermute x11, waiting for transfers between devices, chan_shift(): return lax.ppermute(block, CHAN, pairs)  16.3 us
    all_to_all x1, waiting for transfers between devices, layer(): mixer = lax.all_to_all(mixer, SEQ + ('yh',), 0, 0, tiled=True)  10.8 us
    all_to_all x1, waiting for transfers between devices, layer(): proj = lax.all_to_all(proj, SEQ, 0, 0, tiled=True)  10 us
    pallas_call x7, Pallas kernels, call(): pl.pallas_call(body, out_shape=out_shape, in_specs=[pl.BlockSpec(memory_s...  9.88 us
    all_to_all x1, starting transfers between devices, layer(): proj = lax.all_to_all(proj, SEQ, 0, 0, tiled=True)  9.64 us
    all_to_all x1, starting transfers between devices, layer(): mixer = lax.all_to_all(mixer, SEQ + ('yh',), 0, 0, tiled=True)  5.33 us
  transfers between devices with their start and end apart: 14, of which 6 were waited for; matrix products, arithmetic and copies ran while one was open for 0% of the time, Pallas kernels for 8%

profile of v2, /device:TPU:2, one launch (start us, length us, event | category | flops | bytes accessed | tf_op | source)
XLA Modules:
  0.0 81.6 jit_solution(5147354345114330213)
XLA Ops:
  0.1 1.7 %shard_map.69 = bf16[4,128,512]{2,1,0:T(8,128)(2,1)S(1)} custom-call(s32[2]{0:T(128)S(1)} %pad_add_fusion.index, bf16[256,4096]{1,0:T(8,128)(2,1)} %w_ref.1), custom_call_target="tpu_custom_call" | custom-call | flops 1 | bytes 1048576 | tf_op jit(solution)/shard_map/pallas_call | solution.py:28
  1.8 3.3 %collective-permute-start.7 = (bf16[4,128,512]{2,1,0:T(8,128)(2,1)S(1)}, bf16[4,128,512]{2,1,0:T(8,128)(2,1)}, u32[]{:S(2)}, u32[]{:S(2)}) collective-permute-start(bf16[4,128,512]{2,1,0:T(8,128)(2,1)S(1)} %shard_map.69), channel_id=1, source_target_pairs={{0,1},{1,0},{2,3},{3,2},{4,5},{5,4},{6,7},{7,6},{8,9},{9,8},{10,11... | collective-permute-start | bytes 1572872 | tf_op jit(solution)/shard_map/ppermute | solution.py:23
  5.4 2.1 %collective-permute-start.1 = (bf16[128,512]{1,0:T(8,128)(2,1)S(1)}, bf16[128,512]{1,0:T(8,128)(2,1)S(1)}, u32[]{:S(2)}, u32[]{:S(2)}) collective-permute-start(bf16[128,512]{1,0:T(8,128)(2,1)S(1)} %copy-done.2), channel_id=1, source_target_pairs={{0,4},{1,5},{2,6},{3,7},{4,0},{5,1},{6,2},{7,3},{8,12},{9,13},{10,... | collective-permute-start | bytes 393224 | tf_op jit(solution)/shard_map/ppermute | solution.py:23
  7.5 1.6 %collective-permute-start.2 = (bf16[128,512]{1,0:T(8,128)(2,1)S(1)}, bf16[128,512]{1,0:T(8,128)(2,1)S(1)}, u32[]{:S(2)}, u32[]{:S(2)}) collective-permute-start(bf16[128,512]{1,0:T(8,128)(2,1)S(1)} %copy-done.2), channel_id=1, source_target_pairs={{0,2},{1,3},{2,4},{3,5},{4,6},{5,7},{6,0},{7,1},{8,10},{9,11},{10,... | collective-permute-start | bytes 393224 | tf_op jit(solution)/shard_map/ppermute | solution.py:23
  9.5 10.3 %collective-permute-done.refs_1_ = bf16[128,512]{1,0:T(8,128)(2,1)S(1)} collective-permute-done((bf16[128,512]{1,0:T(8,128)(2,1)S(1)}, bf16[128,512]{1,0:T(8,128)(2,1)S(1)}, u32[]{:S(2)}, u32[]{:S(2)}) %collective-permute-start) | collective-permute-done | bytes 131104 | tf_op jit(solution)/shard_map/ppermute | solution.py:23
  19.8 1.5 %collective-permute-start.5 = (bf16[128,512]{1,0:T(8,128)(2,1)S(1)}, bf16[128,512]{1,0:T(8,128)(2,1)S(1)}, u32[]{:S(2)}, u32[]{:S(2)}) collective-permute-start(bf16[128,512]{1,0:T(8,128)(2,1)S(1)} %collective-permute-done.refs_1_), channel_id=1, source_target_pairs={{0,2},{1,3},{2,4},{3,5},{4,6},{5,7},{6,0},{7,1},{8,10},{9,11},{10,... | collective-permute-start | bytes 393224 | tf_op jit(solution)/shard_map/ppermute | solution.py:23
  21.3 0.5 collective-permute-start.6
  21.9 3.2 %collective-permute-start.4 = (bf16[128,512]{1,0:T(8,128)(2,1)S(1)}, bf16[128,512]{1,0:T(8,128)(2,1)S(1)}, u32[]{:S(2)}, u32[]{:S(2)}) collective-permute-start(bf16[128,512]{1,0:T(8,128)(2,1)S(1)} %collective-permute-done.1.refs_2_), channel_id=1, source_target_pairs={{0,1},{1,0},{2,3},{3,2},{4,5},{5,4},{6,7},{7,6},{8,9},{9,8},{10,11... | collective-permute-start | bytes 393224 | tf_op jit(solution)/shard_map/ppermute | solution.py:23
  25.1 3.5 %shard_map.64 = (f32[3,128,256]{2,1,0:T(8,128)S(1)}, bf16[3,3,512,256]{3,2,1,0:T(8,128)(2,1)S(1)}) custom-call(s32[8]{0:T(128)S(1)} %concatenate.3.order, bf16[3,8,512,256]{3,2,1,0:T(8,128)(2,1)} %bitcast.25, bf16[128,512]{1,0:T(8,128)(2,1)S(1)} %copy-done.2, bf16[128,512]{1,0:T(8,128)(2,1)S(1)} %collective-permute-done.refs_1_, ...), custom_call_target="tpu_custom_call" | custom-call | flops 268435456 | bytes 3145728 | tf_op jit(solution)/shard_map/pallas_call | solution.py:28
  28.7 1.2 %shard_map.65 = bf16[32,3,8,128]{3,2,1,0:T(8,128)(2,1)} custom-call(bf16[3,3,512,256]{3,2,1,0:T(8,128)(2,1)S(1)} %get-tuple-element.13.w_ref, bf16[128,512]{1,0:T(8,128)(2,1)S(1)} %collective-permute-done.4.refs_0_, bf16[128,512]{1,0:T(8,128)(2,1)S(1)} %collective-permute-done.5.refs_1_, bf16[128,512]{1,0:T(8,128)(2,1)S(1)} %collective-permute-done.6.refs_2_, ...), custom_call_target="tpu_custom_call" | custom-call | flops 268435456 | bytes 3145728 | tf_op jit(solution)/shard_map/pallas_call | solution.py:28
  29.9 9.6 %all-to-all-start = ((bf16[32,3,8,128]{3,2,1,0:T(8,128)(2,1)}), bf16[32,3,8,128]{3,2,1,0:T(8,128)(2,1)S(1)}, u32[]{:S(2)}, u32[]{:S(2)}) async-start(bf16[32,3,8,128]{3,2,1,0:T(8,128)(2,1)} %shard_map.65), calls=%async_computation | async-start | bytes 393216 | tf_op jit(solution)/shard_map/all_to_all | solution.py:236
  40.0 1.0 %copy-done.1 = f32[16,4096]{1,0:T(8,128)S(1)} copy-done((f32[16,4096]{1,0:T(8,128)S(1)}, f32[16,4096]{1,0:T(8,128)}, u32[]{:S(2)}) %copy-start.1) | copy-done | bytes 262168
  41.4 10.0 %all-to-all-done.proj_ref = bf16[32,3,8,128]{3,2,1,0:T(8,128)(2,1)S(1)} async-done(((bf16[32,3,8,128]{3,2,1,0:T(8,128)(2,1)}), bf16[32,3,8,128]{3,2,1,0:T(8,128)(2,1)S(1)}, u32[]{:S(2)}, u32[]{:S(2)}) %all-to-all-start) | async-done | bytes 196640 | tf_op jit(solution)/shard_map/all_to_all | solution.py:236
  51.4 1.2 %shard_map.68 = bf16[32,2,8,128]{3,2,1,0:T(8,128)(2,1)} custom-call(bf16[32,3,8,128]{3,2,1,0:T(8,128)(2,1)S(1)} %all-to-all-done.proj_ref, f32[3,3,8,128]{3,2,1,0:T(8,128)S(1)} %get-tuple-element.15.short_ref, f32[8,128]{1,0:T(8,128)S(1)} %get-tuple-element.16.gain_ref, bf16[4096,128]{1,0:T(8,128)(2,1)S(1)} %shard_map.67.lags_ref), custom_call_target="tpu_custom_call" | custom-call | flops 134217728 | bytes 2097152 | tf_op jit(solution)/shard_map/pallas_call | solution.py:28
  52.6 5.3 %all-to-all-start.1 = ((bf16[64,8,128]{2,1,0:T(8,128)(2,1)}), bf16[64,8,128]{2,1,0:T(8,128)(2,1)S(1)}, u32[]{:S(2)}, u32[]{:S(2)}) async-start(bf16[64,8,128]{2,1,0:T(8,128)(2,1)} %bitcast.19), calls=%async_computation.1 | async-start | bytes 262144 | tf_op jit(solution)/shard_map/all_to_all | solution.py:247
  58.0 10.8 %all-to-all-done.1 = bf16[64,8,128]{2,1,0:T(8,128)(2,1)S(1)} async-done(((bf16[64,8,128]{2,1,0:T(8,128)(2,1)}), bf16[64,8,128]{2,1,0:T(8,128)(2,1)S(1)}, u32[]{:S(2)}, u32[]{:S(2)}) %all-to-all-start.1) | async-done | bytes 131104 | tf_op jit(solution)/shard_map/all_to_all | solution.py:247
  68.8 1.8 %shard_map.70 = (bf16[128,512]{1,0:T(8,128)(2,1)S(1)}, bf16[128,512]{1,0:T(8,128)(2,1)S(1)}, bf16[128,512]{1,0:T(8,128)(2,1)S(1)}, f32[128,512]{1,0:T(8,128)S(1)}) custom-call(s32[6]{0:T(128)S(1)} %stack.58.index, bf16[32,2,8,128]{3,2,1,0:T(8,128)(2,1)S(1)} %bitcast.23, bf16[256,4096]{1,0:T(8,128)(2,1)S(1)} %copy-done, ...), custom_call_target="tpu_custom_call" | custom-call | flops 268435456 | bytes 2097152 | tf_op jit(solution)/shard_map/pallas_call | solution.py:28
  70.7 1.6 %collective-permute-start.10 = (bf16[128,512]{1,0:T(8,128)(2,1)S(1)}, bf16[128,512]{1,0:T(8,128)(2,1)S(1)}, u32[]{:S(2)}, u32[]{:S(2)}) collective-permute-start(bf16[128,512]{1,0:T(8,128)(2,1)S(1)} %get-tuple-element.19), channel_id=1, source_target_pairs={{0,2},{1,3},{2,4},{3,5},{4,6},{5,7},{6,0},{7,1},{8,10},{9,11},{10,... | collective-permute-start | bytes 393224 | tf_op jit(solution)/shard_map/ppermute | solution.py:23
  72.2 0.5 collective-permute-start.11
  72.8 2.1 %collective-permute-start.9 = (bf16[128,512]{1,0:T(8,128)(2,1)S(1)}, bf16[128,512]{1,0:T(8,128)(2,1)S(1)}, u32[]{:S(2)}, u32[]{:S(2)}) collective-permute-start(bf16[128,512]{1,0:T(8,128)(2,1)S(1)} %get-tuple-element.18), channel_id=1, source_target_pairs={{0,4},{1,5},{2,6},{3,7},{4,0},{5,1},{6,2},{7,3},{8,12},{9,13},{10,... | collective-permute-start | bytes 393224 | tf_op jit(solution)/shard_map/ppermute | solution.py:23
  74.9 1.4 %collective-permute-done.10 = bf16[128,512]{1,0:T(8,128)(2,1)S(1)} collective-permute-done((bf16[128,512]{1,0:T(8,128)(2,1)S(1)}, bf16[128,512]{1,0:T(8,128)(2,1)S(1)}, u32[]{:S(2)}, u32[]{:S(2)}) %collective-permute-start.10) | collective-permute-done | bytes 131104 | tf_op jit(solution)/shard_map/ppermute | solution.py:23
  76.3 1.7 %collective-permute-done.11 = bf16[128,512]{1,0:T(8,128)(2,1)S(1)} collective-permute-done((bf16[128,512]{1,0:T(8,128)(2,1)S(1)}, bf16[128,512]{1,0:T(8,128)(2,1)S(1)}, u32[]{:S(2)}, u32[]{:S(2)}) %collective-permute-start.11) | collective-permute-done | bytes 131104 | tf_op jit(solution)/shard_map/ppermute | solution.py:23
  78.0 2.9 %collective-permute-done.9 = bf16[128,512]{1,0:T(8,128)(2,1)S(1)} collective-permute-done((bf16[128,512]{1,0:T(8,128)(2,1)S(1)}, bf16[128,512]{1,0:T(8,128)(2,1)S(1)}, u32[]{:S(2)}, u32[]{:S(2)}) %collective-permute-start.9) | collective-permute-done | bytes 131104 | tf_op jit(solution)/shard_map/ppermute | solution.py:23
  80.9 0.7 add_convert_fusion
  (25 shorter events, 1.9 us)
Async XLA Ops:
  0.0 5.0 %copy-start.2 = (bf16[128,512]{1,0:T(8,128)(2,1)S(1)}, bf16[128,512]{1,0:T(8,128)(2,1)}, u32[]{:S(2)}) copy-start(bf16[128,512]{1,0:T(8,128)(2,1)} %refs_0_.1) | copy-start | bytes 393220
  1.8 37.8 %collective-permute-start.7 = (bf16[4,128,512]{2,1,0:T(8,128)(2,1)S(1)}, bf16[4,128,512]{2,1,0:T(8,128)(2,1)}, u32[]{:S(2)}, u32[]{:S(2)}) collective-permute-start(bf16[4,128,512]{2,1,0:T(8,128)(2,1)S(1)} %shard_map.69), channel_id=1, source_target_pairs={{0,1},{1,0},{2,3},{3,2},{4,5},{5,4},{6,7},{7,6},{8,9},{9,8},{10,11... | collective-permute-start | bytes 1572872 | tf_op jit(solution)/shard_map/ppermute | solution.py:23
  5.0 14.8 %collective-permute-start = (bf16[128,512]{1,0:T(8,128)(2,1)S(1)}, bf16[128,512]{1,0:T(8,128)(2,1)S(1)}, u32[]{:S(2)}, u32[]{:S(2)}) collective-permute-start(bf16[128,512]{1,0:T(8,128)(2,1)S(1)} %copy-done.2), channel_id=1, source_target_pairs={{0,1},{1,0},{2,3},{3,2},{4,5},{5,4},{6,7},{7,6},{8,9},{9,8},{10,11... | collective-permute-start | bytes 393224 | tf_op jit(solution)/shard_map/ppermute | solution.py:23
  5.4 15.9 %collective-permute-start.1 = (bf16[128,512]{1,0:T(8,128)(2,1)S(1)}, bf16[128,512]{1,0:T(8,128)(2,1)S(1)}, u32[]{:S(2)}, u32[]{:S(2)}) collective-permute-start(bf16[128,512]{1,0:T(8,128)(2,1)S(1)} %copy-done.2), channel_id=1, source_target_pairs={{0,4},{1,5},{2,6},{3,7},{4,0},{5,1},{6,2},{7,3},{8,12},{9,13},{10,... | collective-permute-start | bytes 393224 | tf_op jit(solution)/shard_map/ppermute | solution.py:23
  7.5 14.4 %collective-permute-start.2 = (bf16[128,512]{1,0:T(8,128)(2,1)S(1)}, bf16[128,512]{1,0:T(8,128)(2,1)S(1)}, u32[]{:S(2)}, u32[]{:S(2)}) collective-permute-start(bf16[128,512]{1,0:T(8,128)(2,1)S(1)} %copy-done.2), channel_id=1, source_target_pairs={{0,2},{1,3},{2,4},{3,5},{4,6},{5,7},{6,0},{7,1},{8,10},{9,11},{10,... | collective-permute-start | bytes 393224 | tf_op jit(solution)/shard_map/ppermute | solution.py:23
  9.1 16.1 %collective-permute-start.3 = (bf16[128,512]{1,0:T(8,128)(2,1)S(1)}, bf16[128,512]{1,0:T(8,128)(2,1)S(1)}, u32[]{:S(2)}, u32[]{:S(2)}) collective-permute-start(bf16[128,512]{1,0:T(8,128)(2,1)S(1)} %copy-done.2), channel_id=1, source_target_pairs={{0,6},{1,7},{2,0},{3,1},{4,2},{5,3},{6,4},{7,5},{8,14},{9,15},{10,... | collective-permute-start | bytes 393224 | tf_op jit(solution)/shard_map/ppermute | solution.py:23
  19.8 8.8 %collective-permute-start.5 = (bf16[128,512]{1,0:T(8,128)(2,1)S(1)}, bf16[128,512]{1,0:T(8,128)(2,1)S(1)}, u32[]{:S(2)}, u32[]{:S(2)}) collective-permute-start(bf16[128,512]{1,0:T(8,128)(2,1)S(1)} %collective-permute-done.refs_1_), channel_id=1, source_target_pairs={{0,2},{1,3},{2,4},{3,5},{4,6},{5,7},{6,0},{7,1},{8,10},{9,11},{10,... | collective-permute-start | bytes 393224 | tf_op jit(solution)/shard_map/ppermute | solution.py:23
  21.3 7.4 %collective-permute-start.6 = (bf16[128,512]{1,0:T(8,128)(2,1)S(1)}, bf16[128,512]{1,0:T(8,128)(2,1)S(1)}, u32[]{:S(2)}, u32[]{:S(2)}) collective-permute-start(bf16[128,512]{1,0:T(8,128)(2,1)S(1)} %collective-permute-done.refs_1_), channel_id=1, source_target_pairs={{0,6},{1,7},{2,0},{3,1},{4,2},{5,3},{6,4},{7,5},{8,14},{9,15},{10,... | collective-permute-start | bytes 393224 | tf_op jit(solution)/shard_map/ppermute | solution.py:23
  21.9 6.8 %collective-permute-start.4 = (bf16[128,512]{1,0:T(8,128)(2,1)S(1)}, bf16[128,512]{1,0:T(8,128)(2,1)S(1)}, u32[]{:S(2)}, u32[]{:S(2)}) collective-permute-start(bf16[128,512]{1,0:T(8,128)(2,1)S(1)} %collective-permute-done.1.refs_2_), channel_id=1, source_target_pairs={{0,1},{1,0},{2,3},{3,2},{4,5},{5,4},{6,7},{7,6},{8,9},{9,8},{10,11... | collective-permute-start | bytes 393224 | tf_op jit(solution)/shard_map/ppermute | solution.py:23
  28.6 11.3 %copy-start.3 = (f32[3,3,256]{2,1,0:T(4,128)S(1)}, f32[3,3,256]{2,1,0:T(4,128)}, u32[]{:S(2)}) copy-start(f32[3,3,256]{2,1,0:T(4,128)} %taps_ref.1) | copy-start | bytes 27652
  28.6 11.3 %copy-start.4 = (f32[256]{0:T(256)S(1)}, f32[256]{0:T(256)}, u32[]{:S(2)}) copy-start(f32[256]{0:T(256)} %param.9) | copy-start | bytes 3076
  29.9 38.9 %copy-start = (bf16[256,4096]{1,0:T(8,128)(2,1)S(1)}, bf16[256,4096]{1,0:T(8,128)(2,1)}, u32[]{:S(2)}) copy-start(bf16[256,4096]{1,0:T(8,128)(2,1)} %w_ref.1) | copy-start | bytes 6291460
  29.9 21.4 %all-to-all-start = ((bf16[32,3,8,128]{3,2,1,0:T(8,128)(2,1)}), bf16[32,3,8,128]{3,2,1,0:T(8,128)(2,1)S(1)}, u32[]{:S(2)}, u32[]{:S(2)}) async-start(bf16[32,3,8,128]{3,2,1,0:T(8,128)(2,1)} %shard_map.65), calls=%async_computation | async-start | bytes 393216 | tf_op jit(solution)/shard_map/all_to_all | solution.py:236
  39.6 29.2 %collective-permute-start.8 = (bf16[4,128,512]{2,1,0:T(8,128)(2,1)}, bf16[4,128,512]{2,1,0:T(8,128)(2,1)}, u32[]{:S(2)}, u32[]{:S(2)}) collective-permute-start(bf16[4,128,512]{2,1,0:T(8,128)(2,1)} %collective-permute-done.7.half_ref), channel_id=1, source_target_pairs={{0,8},{8,0},{1,9},{9,1},{2,10},{10,2},{3,11},{11,3},{4,12},{12,4},... | collective-permute-start | bytes 1572872 | tf_op jit(solution)/shard_map/ppermute | solution.py:235
  40.0 1.0 %copy-start.1 = (f32[16,4096]{1,0:T(8,128)S(1)}, f32[16,4096]{1,0:T(8,128)}, u32[]{:S(2)}) copy-start(f32[16,4096]{1,0:T(8,128)} %filters_ref.1) | copy-start | bytes 786436
  52.6 16.2 %all-to-all-start.1 = ((bf16[64,8,128]{2,1,0:T(8,128)(2,1)}), bf16[64,8,128]{2,1,0:T(8,128)(2,1)S(1)}, u32[]{:S(2)}, u32[]{:S(2)}) async-start(bf16[64,8,128]{2,1,0:T(8,128)(2,1)} %bitcast.19), calls=%async_computation.1 | async-start | bytes 262144 | tf_op jit(solution)/shard_map/all_to_all | solution.py:247
  70.7 5.6 %collective-permute-start.10 = (bf16[128,512]{1,0:T(8,128)(2,1)S(1)}, bf16[128,512]{1,0:T(8,128)(2,1)S(1)}, u32[]{:S(2)}, u32[]{:S(2)}) collective-permute-start(bf16[128,512]{1,0:T(8,128)(2,1)S(1)} %get-tuple-element.19), channel_id=1, source_target_pairs={{0,2},{1,3},{2,4},{3,5},{4,6},{5,7},{6,0},{7,1},{8,10},{9,11},{10,... | collective-permute-start | bytes 393224 | tf_op jit(solution)/shard_map/ppermute | solution.py:23
  72.2 5.7 %collective-permute-start.11 = (bf16[128,512]{1,0:T(8,128)(2,1)S(1)}, bf16[128,512]{1,0:T(8,128)(2,1)S(1)}, u32[]{:S(2)}, u32[]{:S(2)}) collective-permute-start(bf16[128,512]{1,0:T(8,128)(2,1)S(1)} %get-tuple-element.20), channel_id=1, source_target_pairs={{0,6},{1,7},{2,0},{3,1},{4,2},{5,3},{6,4},{7,5},{8,14},{9,15},{10,... | collective-permute-start | bytes 393224 | tf_op jit(solution)/shard_map/ppermute | solution.py:23
  72.8 8.1 %collective-permute-start.9 = (bf16[128,512]{1,0:T(8,128)(2,1)S(1)}, bf16[128,512]{1,0:T(8,128)(2,1)S(1)}, u32[]{:S(2)}, u32[]{:S(2)}) collective-permute-start(bf16[128,512]{1,0:T(8,128)(2,1)S(1)} %get-tuple-element.18), channel_id=1, source_target_pairs={{0,4},{1,5},{2,6},{3,7},{4,0},{5,1},{6,2},{7,3},{8,12},{9,13},{10,... | collective-permute-start | bytes 393224 | tf_op jit(solution)/shard_map/ppermute | solution.py:23

commit v3 on v2

--- a/solution.py
+++ b/solution.py
@@ -1,3 +1,5 @@
+import functools
+
 import jax
 import jax.numpy as jnp
 from jax import lax
@@ -76,8 +78,8 @@
 
 
 def columns_body(index, w_hbm, out_ref, sem):
-    parts, half, feats = out_ref.shape
-    rows, loads = pl.ds(pl.multiple_of(index[1] * half, half), half), []
+    parts, count, feats = out_ref.shape
+    rows, loads = pl.ds(pl.multiple_of(index[1] * count, count), count), []
     for x in range(parts):
         start = pl.multiple_of((2 * x + index[0]) * feats, feats)
         loads.append(pltpu.make_async_copy(w_hbm.at[rows, pl.ds(start, feats)], out_ref.at[x], sem.at[x]))
@@ -100,12 +102,18 @@
         load.wait()
 
 
-def project_far_body(w_ref, *refs):
+def project_mid_body(skip, w_ref, *refs):
     blocks, (before_ref, out_ref) = refs[:-2], refs[-2:]
     for k in range(w_ref.shape[1]):
         total = before_ref[k]
         for i, block in enumerate(blocks):
-            total = total + jnp.dot(block[...], w_ref[i, k], preferred_element_type=jnp.float32)
+            total = total + jnp.dot(block[...], w_ref[skip + i, k], preferred_element_type=jnp.float32)
+        out_ref[k] = total
+
+
+def project_far_body(w_ref, block, before_ref, out_ref):
+    for k in range(w_ref.shape[1]):
+        total = before_ref[k] + jnp.dot(block[...], w_ref[0, k], preferred_element_type=jnp.float32)
         turned = total.T.reshape(out_ref.shape[0], out_ref.shape[2], out_ref.shape[3])
         out_ref[:, k] = turned.astype(jnp.bfloat16)
 
@@ -144,10 +152,17 @@
         out_ref[:, y] = mixed
 
 
-def output_body(index, mixer_ref, w_ref, half_ref, twin_ref, *outs):
+def output_body(index, half_hbm, twin_hbm, mixer_ref, w_ref, *refs):
+    outs, (half_ref, twin_ref, total_ref, sem) = refs[:-4], refs[-4:]
+    loads = [
+        pltpu.make_async_copy(half_hbm, half_ref, sem.at[0]),
+        pltpu.make_async_copy(twin_hbm, twin_ref, sem.at[1]),
+    ]
+    for load in loads:
+        load.start()
     iy, core = index[0], index[1]
-    count, ny, per, rows = mixer_ref.shape
-    half, feats = count // 2, outs[0].shape[1]
+    count, _, per, rows = mixer_ref.shape
+    half = count // 2
 
     def mixer_of(block):
         block = block.astype(jnp.float32)
@@ -156,11 +171,13 @@
     mine = mixer_of(mixer_ref[:, iy])
     here = mixer_of(mixer_ref[pl.ds(core * half, half), 1 - iy])
     there = mixer_of(mixer_ref[pl.ds((1 - core) * half, half), 1 - iy])
+    for i in range(len(outs)):
+        total_ref[i] = jnp.dot(mine, w_ref[index[2 + i]], preferred_element_type=jnp.float32)
+    for load in loads:
+        load.wait()
     for i, out in enumerate(outs):
         x = index[2 + i]
-        start = pl.multiple_of((ny * x + iy) * feats, feats)
-        total = jnp.dot(mine, w_ref[:, pl.ds(start, feats)], preferred_element_type=jnp.float32)
-        total = total + jnp.dot(here, half_ref[x], preferred_element_type=jnp.float32)
+        total = total_ref[i] + jnp.dot(here, half_ref[x], preferred_element_type=jnp.float32)
         total = total + jnp.dot(there, twin_ref[x], preferred_element_type=jnp.float32)
         out[...] = total.astype(out.dtype)
 
@@ -202,14 +219,13 @@
         near.append(chan_shift(tokens, d, 0))
     for d in steps:
         far.append(chan_shift(near[0], 0, 1) if d == 2 else chan_shift(across, d, 0))
-    at_first = jnp.stack([ix * ny + iy, ix * ny + 1 - iy])
     at_near = jnp.stack([x_of(-d) * ny + iy for d in steps])
     at_far = jnp.stack([x_of(-d) * ny + 1 - iy for d in steps])
     work = dict(flops=2 * rows * width * kinds * chan_dev // 3, nbytes=width * kinds * chan_dev)
     partial = shape((kinds, rows, chan_dev), f32)
-    order = jnp.concatenate([at_first, at_near, at_far])
+    order = jnp.concatenate([ix[None] * ny + 1 - iy, at_near, at_far, ix[None] * ny + iy])
     chunk = (kinds, feats, chan_dev)
-    first, dma = 2 + len(steps), pltpu.SemaphoreType.DMA
+    first, dma = 1 + len(steps), pltpu.SemaphoreType.DMA
     columns = call(
         columns_body,
         shape((nx, chan_dev // 2, feats), bf),
@@ -221,17 +237,16 @@
     )
     acc, w_next = call(
         project_near_body,
-        [partial, shape((len(steps),) + chunk, bf)],
-        [order, w3, tokens, across] + near,
+        [partial, shape((first,) + chunk, bf)],
+        [order, w3, across] + near,
         "sh",
-        scratch=[pltpu.VMEM((first,) + chunk, bf), dma((first,)), dma((len(steps),))],
+        scratch=[pltpu.VMEM((first,) + chunk, bf), dma((first,)), dma((first,))],
         vmem=48,
         **work,
     )
-    proj = call(
-        project_far_body, shape((n_seq, kinds, per, rows), bf), [w_next] + far + [acc], "", **work
-    )
-    columns = chan_shift(columns, 0, 1)
+    acc = call(functools.partial(project_mid_body, 1), partial, [w_next] + far[1:] + [tokens, acc], "", **work)
+    proj = call(project_far_body, shape((n_seq, kinds, per, rows), bf), [w_next, far[0], acc], "", **work)
+    columns = lax.ppermute(columns, ("yl", "yh"), [(i, 3 - i) for i in range(4)])
     twin = lax.ppermute(columns, "core", [(0, 1), (1, 0)])
     proj = lax.all_to_all(proj, SEQ, 0, 0, tiled=True)
     mixer = call(
@@ -246,12 +261,26 @@
     mixer = mixer.reshape(n_seq * ny, per, rows)
     mixer = lax.all_to_all(mixer, SEQ + ("yh",), 0, 0, tiled=True)
     mixer = mixer.reshape(n_seq, ny, per, rows)
+    own_columns = call(
+        columns_body,
+        shape((nx, chan_dev, feats), bf),
+        [jnp.stack([iy, 0 * iy]), w_out],
+        "sh",
+        scratch=[dma((nx,))],
+        nbytes=chan_dev * width,
+    )
     block, wide = shape((rows, feats), bf), shape((rows, feats), f32)
     sends = call(
         output_body,
         [block] * (nx - 1) + [wide],
-        [jnp.stack([iy, core] + [x_of(d) for d in steps + [0]]), mixer, w_out, columns, twin],
-        "s",
+        [jnp.stack([iy, core] + [x_of(d) for d in steps + [0]]), columns, twin, mixer, own_columns],
+        "shh",
+        scratch=[
+            pltpu.VMEM(columns.shape, bf),
+            pltpu.VMEM(columns.shape, bf),
+            pltpu.VMEM((nx, rows, feats), f32),
+            dma((2,)),
+        ],
         flops=2 * rows * chan_dev * width,
         nbytes=2 * chan_dev * width,
     )

time: 82.7 us -> 75.3 us (0.911)
  waiting for transfers between devices: 37.1 us -> 30.8 us
  starting transfers between devices: 32.5 us -> 29.9 us
  Pallas kernels: 9.88 us -> 11.3 us
    ppermute x11 -> x10, waiting for transfers between devices: 16.3 us -> 10.8 us  [chan_shift(): return lax.ppermute(block, CHAN, pairs)]
    ppermute x11 -> x10, starting transfers between devices: 17.2 us -> 12.6 us  [chan_shift(): return lax.ppermute(block, CHAN, pairs)]
    ppermute x0 -> x1, starting transfers between devices: none -> 3.1 us  [layer(): lax.ppermute(columns, ('yl', 'yh'), [(i, 3 - i) for i in range(4)])]
    pallas_call x7 -> x9, Pallas kernels: 9.88 us -> 11.3 us  [call(): pl.pallas_call(body, out_shape=out_shape, in_specs=[pl.BlockSpec(memory_s...]
  transfers between devices with their start and end apart: 14 -> 14, of which waited for: 6 -> 7; matrix products, arithmetic and copies ran while one was open for 0% -> 0% of each run, Pallas kernels for 8% -> 10%
where the time goes in v3:
time: 75.3 us; the launch traced here: 74.2 us
  waiting for transfers between devices  30.8 us (41%)
  starting transfers between devices  29.9 us (40%)
  Pallas kernels  11.3 us (15%)
  local copies, waits for them, and re-layouts  1.15 us (2%)
  other arithmetic  0.87 us (1%)
    ppermute x10, starting transfers between devices, chan_shift(): return lax.ppermute(block, CHAN, pairs)  12.6 us
    pallas_call x9, Pallas kernels, call(): pl.pallas_call(body, out_shape=out_shape, in_specs=[pl.BlockSpec(memory_s...  11.3 us
    ppermute x10, waiting for transfers between devices, chan_shift(): return lax.ppermute(block, CHAN, pairs)  10.8 us
    all_to_all x1, waiting for transfers between devices, layer(): mixer = lax.all_to_all(mixer, SEQ + ('yh',), 0, 0, tiled=True)  10 us
    all_to_all x1, waiting for transfers between devices, layer(): proj = lax.all_to_all(proj, SEQ, 0, 0, tiled=True)  10 us
    all_to_all x1, starting transfers between devices, layer(): proj = lax.all_to_all(proj, SEQ, 0, 0, tiled=True)  8.86 us
    all_to_all x1, starting transfers between devices, layer(): mixer = lax.all_to_all(mixer, SEQ + ('yh',), 0, 0, tiled=True)  5.03 us
    ppermute x1, starting transfers between devices, layer(): lax.ppermute(columns, ('yl', 'yh'), [(i, 3 - i) for i in range(4)])  3.1 us
  transfers between devices with their start and end apart: 14, of which 7 were waited for; matrix products, arithmetic and copies ran while one was open for 0% of the time, Pallas kernels for 10%

profile of v3, /device:TPU:2, one launch (start us, length us, event | category | flops | bytes accessed | tf_op | source)
XLA Modules:
  0.0 74.2 jit_solution(14099207252060213075)
XLA Ops:
  0.1 1.7 %shard_map.64 = bf16[4,128,512]{2,1,0:T(8,128)(2,1)S(1)} custom-call(s32[2]{0:T(128)S(1)} %pad_add_fusion.index, bf16[256,4096]{1,0:T(8,128)(2,1)} %w_hbm.3), custom_call_target="tpu_custom_call" | custom-call | flops 1 | bytes 1048576 | tf_op jit(solution)/shard_map/pallas_call | solution.py:30
  1.8 3.1 %collective-permute-start = (bf16[4,128,512]{2,1,0:T(8,128)(2,1)S(1)}, bf16[4,128,512]{2,1,0:T(8,128)(2,1)}, u32[]{:S(2)}, u32[]{:S(2)}) collective-permute-start(bf16[4,128,512]{2,1,0:T(8,128)(2,1)S(1)} %shard_map.64), channel_id=1, source_target_pairs={{0,129},{1,128},{128,1},{129,0},{2,131},{3,130},{130,3},{131,2},{4... | collective-permute-start | bytes 1572872 | tf_op jit(solution)/shard_map/ppermute | solution.py:249
  4.9 0.6 collective-permute-start.2
  5.5 2.1 %collective-permute-start.3 = (bf16[128,512]{1,0:T(8,128)(2,1)}, bf16[128,512]{1,0:T(8,128)(2,1)S(1)}, u32[]{:S(2)}, u32[]{:S(2)}) collective-permute-start(bf16[128,512]{1,0:T(8,128)(2,1)} %refs_2_.1), channel_id=1, source_target_pairs={{0,4},{1,5},{2,6},{3,7},{4,0},{5,1},{6,2},{7,3},{8,12},{9,13},{10,... | collective-permute-start | bytes 393224 | tf_op jit(solution)/shard_map/ppermute | solution.py:25
  7.6 2.0 %collective-permute-start.5 = (bf16[128,512]{1,0:T(8,128)(2,1)}, bf16[128,512]{1,0:T(8,128)(2,1)S(1)}, u32[]{:S(2)}, u32[]{:S(2)}) collective-permute-start(bf16[128,512]{1,0:T(8,128)(2,1)} %refs_2_.1), channel_id=1, source_target_pairs={{0,6},{1,7},{2,0},{3,1},{4,2},{5,3},{6,4},{7,5},{8,14},{9,15},{10,... | collective-permute-start | bytes 393224 | tf_op jit(solution)/shard_map/ppermute | solution.py:25
  9.6 2.0 %collective-permute-done.2.refs_0_ = bf16[128,512]{1,0:T(8,128)(2,1)S(1)} collective-permute-done((bf16[128,512]{1,0:T(8,128)(2,1)}, bf16[128,512]{1,0:T(8,128)(2,1)S(1)}, u32[]{:S(2)}, u32[]{:S(2)}) %collective-permute-start.2) | collective-permute-done | bytes 131104 | tf_op jit(solution)/shard_map/ppermute | solution.py:25
  11.6 1.5 %collective-permute-start.7 = (bf16[128,512]{1,0:T(8,128)(2,1)S(1)}, bf16[128,512]{1,0:T(8,128)(2,1)S(1)}, u32[]{:S(2)}, u32[]{:S(2)}) collective-permute-start(bf16[128,512]{1,0:T(8,128)(2,1)S(1)} %collective-permute-done.2.refs_0_), channel_id=1, source_target_pairs={{0,2},{1,3},{2,4},{3,5},{4,6},{5,7},{6,0},{7,1},{8,10},{9,11},{10,... | collective-permute-start | bytes 393224 | tf_op jit(solution)/shard_map/ppermute | solution.py:25
  14.0 2.2 %collective-permute-done.4.refs_2_ = bf16[128,512]{1,0:T(8,128)(2,1)S(1)} collective-permute-done((bf16[128,512]{1,0:T(8,128)(2,1)}, bf16[128,512]{1,0:T(8,128)(2,1)S(1)}, u32[]{:S(2)}, u32[]{:S(2)}) %collective-permute-start.4) | collective-permute-done | bytes 131104 | tf_op jit(solution)/shard_map/ppermute | solution.py:25
  16.2 2.9 %collective-permute-start.6 = (bf16[128,512]{1,0:T(8,128)(2,1)S(1)}, bf16[128,512]{1,0:T(8,128)(2,1)S(1)}, u32[]{:S(2)}, u32[]{:S(2)}) collective-permute-start(bf16[128,512]{1,0:T(8,128)(2,1)S(1)} %collective-permute-done.3.refs_1_), channel_id=1, source_target_pairs={{0,1},{1,0},{2,3},{3,2},{4,5},{5,4},{6,7},{7,6},{8,9},{9,8},{10,11... | collective-permute-start | bytes 393224 | tf_op jit(solution)/shard_map/ppermute | solution.py:25
  19.2 3.5 %shard_map.65 = (f32[3,128,256]{2,1,0:T(8,128)S(1)}, bf16[4,3,512,256]{3,2,1,0:T(8,128)(2,1)S(1)}) custom-call(s32[8]{0:T(128)S(1)} %concatenate.3.order, bf16[3,8,512,256]{3,2,1,0:T(8,128)(2,1)} %bitcast.24, bf16[128,512]{1,0:T(8,128)(2,1)S(1)} %collective-permute-done.2.refs_0_, bf16[128,512]{1,0:T(8,128)(2,1)S(1)} %collective-permute-done.3.refs_1_, ...), custom_call_target="tpu_custom_call" | custom-call | flops 268435456 | bytes 3145728 | tf_op jit(solution)/shard_map/pallas_call | solution.py:30
  23.2 1.0 %shard_map.67 = bf16[32,3,8,128]{3,2,1,0:T(8,128)(2,1)} custom-call(bf16[4,3,512,256]{3,2,1,0:T(8,128)(2,1)S(1)} %get-tuple-element.13.w_ref, bf16[128,512]{1,0:T(8,128)(2,1)S(1)} %collective-permute-done.6.block, f32[3,128,256]{2,1,0:T(8,128)S(1)} %shard_map.66.before_ref), custom_call_target="tpu_custom_call" | custom-call | flops 268435456 | bytes 3145728 | tf_op jit(solution)/shard_map/pallas_call | solution.py:30
  24.3 8.9 %all-to-all-start = ((bf16[32,3,8,128]{3,2,1,0:T(8,128)(2,1)}), bf16[32,3,8,128]{3,2,1,0:T(8,128)(2,1)S(1)}, u32[]{:S(2)}, u32[]{:S(2)}) async-start(bf16[32,3,8,128]{3,2,1,0:T(8,128)(2,1)} %shard_map.67), calls=%async_computation | async-start | bytes 393216 | tf_op jit(solution)/shard_map/all_to_all | solution.py:251
  33.6 1.0 %copy-done.1 = f32[16,4096]{1,0:T(8,128)S(1)} copy-done((f32[16,4096]{1,0:T(8,128)S(1)}, f32[16,4096]{1,0:T(8,128)}, u32[]{:S(2)}) %copy-start.1) | copy-done | bytes 262168
  34.9 10.0 %all-to-all-done.proj_ref = bf16[32,3,8,128]{3,2,1,0:T(8,128)(2,1)S(1)} async-done(((bf16[32,3,8,128]{3,2,1,0:T(8,128)(2,1)}), bf16[32,3,8,128]{3,2,1,0:T(8,128)(2,1)S(1)}, u32[]{:S(2)}, u32[]{:S(2)}) %all-to-all-start) | async-done | bytes 196640 | tf_op jit(solution)/shard_map/all_to_all | solution.py:251
  44.9 1.2 %shard_map.70 = bf16[32,2,8,128]{3,2,1,0:T(8,128)(2,1)} custom-call(bf16[32,3,8,128]{3,2,1,0:T(8,128)(2,1)S(1)} %all-to-all-done.proj_ref, f32[3,3,8,128]{3,2,1,0:T(8,128)S(1)} %get-tuple-element.15.short_ref, f32[8,128]{1,0:T(8,128)S(1)} %get-tuple-element.16.gain_ref, bf16[4096,128]{1,0:T(8,128)(2,1)S(1)} %shard_map.69.lags_ref), custom_call_target="tpu_custom_call" | custom-call | flops 134217728 | bytes 2097152 | tf_op jit(solution)/shard_map/pallas_call | solution.py:30
  46.1 5.0 %all-to-all-start.1 = ((bf16[64,8,128]{2,1,0:T(8,128)(2,1)}), bf16[64,8,128]{2,1,0:T(8,128)(2,1)S(1)}, u32[]{:S(2)}, u32[]{:S(2)}) async-start(bf16[64,8,128]{2,1,0:T(8,128)(2,1)} %bitcast.19), calls=%async_computation.1 | async-start | bytes 262144 | tf_op jit(solution)/shard_map/all_to_all | solution.py:262
  51.2 0.7 shard_map.71.w_ref
  52.0 10.0 %all-to-all-done.1 = bf16[64,8,128]{2,1,0:T(8,128)(2,1)S(1)} async-done(((bf16[64,8,128]{2,1,0:T(8,128)(2,1)}), bf16[64,8,128]{2,1,0:T(8,128)(2,1)S(1)}, u32[]{:S(2)}, u32[]{:S(2)}) %all-to-all-start.1) | async-done | bytes 131104 | tf_op jit(solution)/shard_map/all_to_all | solution.py:262
  62.1 2.3 %shard_map.72 = (bf16[128,512]{1,0:T(8,128)(2,1)S(1)}, bf16[128,512]{1,0:T(8,128)(2,1)S(1)}, bf16[128,512]{1,0:T(8,128)(2,1)S(1)}, f32[128,512]{1,0:T(8,128)S(1)}) custom-call(s32[6]{0:T(128)S(1)} %stack.56.index, bf16[4,128,512]{2,1,0:T(8,128)(2,1)} %collective-permute-done.half_hbm, bf16[4,128,512]{2,1,0:T(8,128)(2,1)} %collective-permute-done.1.twin_hbm, ...), custom_call_target="tpu_custom_call" | custom-call | flops 268435456 | bytes 2097152 | tf_op jit(solution)/shard_map/pallas_call | solution.py:30
  64.5 1.9 %collective-permute-start.11 = (bf16[128,512]{1,0:T(8,128)(2,1)S(1)}, bf16[128,512]{1,0:T(8,128)(2,1)S(1)}, u32[]{:S(2)}, u32[]{:S(2)}) collective-permute-start(bf16[128,512]{1,0:T(8,128)(2,1)S(1)} %get-tuple-element.20), channel_id=1, source_target_pairs={{0,6},{1,7},{2,0},{3,1},{4,2},{5,3},{6,4},{7,5},{8,14},{9,15},{10,... | collective-permute-start | bytes 393224 | tf_op jit(solution)/shard_map/ppermute | solution.py:25
  66.5 0.7 collective-permute-start.9
  67.2 3.6 %collective-permute-done.10 = bf16[128,512]{1,0:T(8,128)(2,1)S(1)} collective-permute-done((bf16[128,512]{1,0:T(8,128)(2,1)S(1)}, bf16[128,512]{1,0:T(8,128)(2,1)S(1)}, u32[]{:S(2)}, u32[]{:S(2)}) %collective-permute-start.10) | collective-permute-done | bytes 131104 | tf_op jit(solution)/shard_map/ppermute | solution.py:25
  70.8 2.7 %collective-permute-done.9 = bf16[128,512]{1,0:T(8,128)(2,1)S(1)} collective-permute-done((bf16[128,512]{1,0:T(8,128)(2,1)S(1)}, bf16[128,512]{1,0:T(8,128)(2,1)S(1)}, u32[]{:S(2)}, u32[]{:S(2)}) %collective-permute-start.9) | collective-permute-done | bytes 131104 | tf_op jit(solution)/shard_map/ppermute | solution.py:25
  73.5 0.7 add_convert_fusion
  (28 shorter events, 2.7 us)
Async XLA Ops:
  1.8 31.4 %collective-permute-start = (bf16[4,128,512]{2,1,0:T(8,128)(2,1)S(1)}, bf16[4,128,512]{2,1,0:T(8,128)(2,1)}, u32[]{:S(2)}, u32[]{:S(2)}) collective-permute-start(bf16[4,128,512]{2,1,0:T(8,128)(2,1)S(1)} %shard_map.64), channel_id=1, source_target_pairs={{0,129},{1,128},{128,1},{129,0},{2,131},{3,130},{130,3},{131,2},{4... | collective-permute-start | bytes 1572872 | tf_op jit(solution)/shard_map/ppermute | solution.py:249
  4.9 6.8 %collective-permute-start.2 = (bf16[128,512]{1,0:T(8,128)(2,1)}, bf16[128,512]{1,0:T(8,128)(2,1)S(1)}, u32[]{:S(2)}, u32[]{:S(2)}) collective-permute-start(bf16[128,512]{1,0:T(8,128)(2,1)} %refs_2_.1), channel_id=1, source_target_pairs={{0,1},{1,0},{2,3},{3,2},{4,5},{5,4},{6,7},{7,6},{8,9},{9,8},{10,11... | collective-permute-start | bytes 393224 | tf_op jit(solution)/shard_map/ppermute | solution.py:25
  5.5 7.9 %collective-permute-start.3 = (bf16[128,512]{1,0:T(8,128)(2,1)}, bf16[128,512]{1,0:T(8,128)(2,1)S(1)}, u32[]{:S(2)}, u32[]{:S(2)}) collective-permute-start(bf16[128,512]{1,0:T(8,128)(2,1)} %refs_2_.1), channel_id=1, source_target_pairs={{0,4},{1,5},{2,6},{3,7},{4,0},{5,1},{6,2},{7,3},{8,12},{9,13},{10,... | collective-permute-start | bytes 393224 | tf_op jit(solution)/shard_map/ppermute | solution.py:25
  7.6 8.6 %collective-permute-start.4 = (bf16[128,512]{1,0:T(8,128)(2,1)}, bf16[128,512]{1,0:T(8,128)(2,1)S(1)}, u32[]{:S(2)}, u32[]{:S(2)}) collective-permute-start(bf16[128,512]{1,0:T(8,128)(2,1)} %refs_2_.1), channel_id=1, source_target_pairs={{0,2},{1,3},{2,4},{3,5},{4,6},{5,7},{6,0},{7,1},{8,10},{9,11},{10,... | collective-permute-start | bytes 393224 | tf_op jit(solution)/shard_map/ppermute | solution.py:25
  7.6 11.5 %collective-permute-start.5 = (bf16[128,512]{1,0:T(8,128)(2,1)}, bf16[128,512]{1,0:T(8,128)(2,1)S(1)}, u32[]{:S(2)}, u32[]{:S(2)}) collective-permute-start(bf16[128,512]{1,0:T(8,128)(2,1)} %refs_2_.1), channel_id=1, source_target_pairs={{0,6},{1,7},{2,0},{3,1},{4,2},{5,3},{6,4},{7,5},{8,14},{9,15},{10,... | collective-permute-start | bytes 393224 | tf_op jit(solution)/shard_map/ppermute | solution.py:25
  11.6 11.0 %collective-permute-start.7 = (bf16[128,512]{1,0:T(8,128)(2,1)S(1)}, bf16[128,512]{1,0:T(8,128)(2,1)S(1)}, u32[]{:S(2)}, u32[]{:S(2)}) collective-permute-start(bf16[128,512]{1,0:T(8,128)(2,1)S(1)} %collective-permute-done.2.refs_0_), channel_id=1, source_target_pairs={{0,2},{1,3},{2,4},{3,5},{4,6},{5,7},{6,0},{7,1},{8,10},{9,11},{10,... | collective-permute-start | bytes 393224 | tf_op jit(solution)/shard_map/ppermute | solution.py:25
  13.4 9.3 %collective-permute-start.8 = (bf16[128,512]{1,0:T(8,128)(2,1)S(1)}, bf16[128,512]{1,0:T(8,128)(2,1)S(1)}, u32[]{:S(2)}, u32[]{:S(2)}) collective-permute-start(bf16[128,512]{1,0:T(8,128)(2,1)S(1)} %collective-permute-done.2.refs_0_), channel_id=1, source_target_pairs={{0,6},{1,7},{2,0},{3,1},{4,2},{5,3},{6,4},{7,5},{8,14},{9,15},{10,... | collective-permute-start | bytes 393224 | tf_op jit(solution)/shard_map/ppermute | solution.py:25
  16.2 7.1 %collective-permute-start.6 = (bf16[128,512]{1,0:T(8,128)(2,1)S(1)}, bf16[128,512]{1,0:T(8,128)(2,1)S(1)}, u32[]{:S(2)}, u32[]{:S(2)}) collective-permute-start(bf16[128,512]{1,0:T(8,128)(2,1)S(1)} %collective-permute-done.3.refs_1_), channel_id=1, source_target_pairs={{0,1},{1,0},{2,3},{3,2},{4,5},{5,4},{6,7},{7,6},{8,9},{9,8},{10,11... | collective-permute-start | bytes 393224 | tf_op jit(solution)/shard_map/ppermute | solution.py:25
  19.2 3.5 %copy-start.2 = (bf16[128,512]{1,0:T(8,128)(2,1)S(1)}, bf16[128,512]{1,0:T(8,128)(2,1)}, u32[]{:S(2)}) copy-start(bf16[128,512]{1,0:T(8,128)(2,1)} %refs_2_.1) | copy-start | bytes 393220
  23.2 10.3 %copy-start.3 = (f32[3,3,256]{2,1,0:T(4,128)S(1)}, f32[3,3,256]{2,1,0:T(4,128)}, u32[]{:S(2)}) copy-start(f32[3,3,256]{2,1,0:T(4,128)} %taps_ref.1) | copy-start | bytes 27652
  23.2 10.3 %copy-start.4 = (f32[256]{0:T(256)S(1)}, f32[256]{0:T(256)}, u32[]{:S(2)}) copy-start(f32[256]{0:T(256)} %param.9) | copy-start | bytes 3076
  23.2 28.0 %copy-start = (bf16[256,4096]{1,0:T(8,128)(2,1)S(1)}, bf16[256,4096]{1,0:T(8,128)(2,1)}, u32[]{:S(2)}) copy-start(bf16[256,4096]{1,0:T(8,128)(2,1)} %w_hbm.3) | copy-start | bytes 6291460
  24.3 20.7 %all-to-all-start = ((bf16[32,3,8,128]{3,2,1,0:T(8,128)(2,1)}), bf16[32,3,8,128]{3,2,1,0:T(8,128)(2,1)S(1)}, u32[]{:S(2)}, u32[]{:S(2)}) async-start(bf16[32,3,8,128]{3,2,1,0:T(8,128)(2,1)} %shard_map.67), calls=%async_computation | async-start | bytes 393216 | tf_op jit(solution)/shard_map/all_to_all | solution.py:251
  33.1 28.9 %collective-permute-start.1 = (bf16[4,128,512]{2,1,0:T(8,128)(2,1)}, bf16[4,128,512]{2,1,0:T(8,128)(2,1)}, u32[]{:S(2)}, u32[]{:S(2)}) collective-permute-start(bf16[4,128,512]{2,1,0:T(8,128)(2,1)} %collective-permute-done.half_hbm), channel_id=1, source_target_pairs={{0,8},{8,0},{1,9},{9,1},{2,10},{10,2},{3,11},{11,3},{4,12},{12,4},... | collective-permute-start | bytes 1572872 | tf_op jit(solution)/shard_map/ppermute | solution.py:250
  33.6 1.0 %copy-start.1 = (f32[16,4096]{1,0:T(8,128)S(1)}, f32[16,4096]{1,0:T(8,128)}, u32[]{:S(2)}) copy-start(f32[16,4096]{1,0:T(8,128)} %filters_ref.1) | copy-start | bytes 786436
  46.1 15.9 %all-to-all-start.1 = ((bf16[64,8,128]{2,1,0:T(8,128)(2,1)}), bf16[64,8,128]{2,1,0:T(8,128)(2,1)S(1)}, u32[]{:S(2)}, u32[]{:S(2)}) async-start(bf16[64,8,128]{2,1,0:T(8,128)(2,1)} %bitcast.19), calls=%async_computation.1 | async-start | bytes 262144 | tf_op jit(solution)/shard_map/all_to_all | solution.py:262
  64.4 6.4 %collective-permute-start.10 = (bf16[128,512]{1,0:T(8,128)(2,1)S(1)}, bf16[128,512]{1,0:T(8,128)(2,1)S(1)}, u32[]{:S(2)}, u32[]{:S(2)}) collective-permute-start(bf16[128,512]{1,0:T(8,128)(2,1)S(1)} %get-tuple-element.19), channel_id=1, source_target_pairs={{0,2},{1,3},{2,4},{3,5},{4,6},{5,7},{6,0},{7,1},{8,10},{9,11},{10,... | collective-permute-start | bytes 393224 | tf_op jit(solution)/shard_map/ppermute | solution.py:25
  64.5 6.3 %collective-permute-start.11 = (bf16[128,512]{1,0:T(8,128)(2,1)S(1)}, bf16[128,512]{1,0:T(8,128)(2,1)S(1)}, u32[]{:S(2)}, u32[]{:S(2)}) collective-permute-start(bf16[128,512]{1,0:T(8,128)(2,1)S(1)} %get-tuple-element.20), channel_id=1, source_target_pairs={{0,6},{1,7},{2,0},{3,1},{4,2},{5,3},{6,4},{7,5},{8,14},{9,15},{10,... | collective-permute-start | bytes 393224 | tf_op jit(solution)/shard_map/ppermute | solution.py:25
  66.5 7.0 %collective-permute-start.9 = (bf16[128,512]{1,0:T(8,128)(2,1)S(1)}, bf16[128,512]{1,0:T(8,128)(2,1)S(1)}, u32[]{:S(2)}, u32[]{:S(2)}) collective-permute-start(bf16[128,512]{1,0:T(8,128)(2,1)S(1)} %get-tuple-element.18), channel_id=1, source_target_pairs={{0,4},{1,5},{2,6},{3,7},{4,0},{5,1},{6,2},{7,3},{8,12},{9,13},{10,... | collective-permute-start | bytes 393224 | tf_op jit(solution)/shard_map/ppermute | solution.py:25

commit v4 on v3

--- a/solution.py
+++ b/solution.py
@@ -88,16 +88,19 @@
         load.wait()
 
 
-def project_near_body(order, w_hbm, *refs):
-    blocks, (out_ref, next_ref, w_ref, sem, next_sem) = refs[:-5], refs[-5:]
-    count = len(blocks)
-    loads = fetch(order, 0, w_hbm, w_ref, sem)
-    later = fetch(order, count, w_hbm, next_ref, next_sem)
-    for i, block in enumerate(blocks):
-        loads[i].wait()
-        for k in range(w_ref.shape[1]):
-            part = jnp.dot(block[...], w_ref[i, k], preferred_element_type=jnp.float32)
-            out_ref[k] = part if i == 0 else out_ref[k] + part
+def fetch_body(order, w_hbm, out_ref, sem):
+    for load in fetch(order, 0, w_hbm, out_ref, sem):
+        load.wait()
+
+
+def project_near_body(order, w_hbm, w_ref, *refs):
+    blocks, (out_ref, next_ref, next_sem) = refs[:-3], refs[-3:]
+    later = fetch(order, len(blocks), w_hbm, next_ref, next_sem)
+    for k in range(w_ref.shape[1]):
+        total = jnp.dot(blocks[0][...], w_ref[0, k], preferred_element_type=jnp.float32)
+        for i, block in enumerate(blocks[1:]):
+            total = total + jnp.dot(block[...], w_ref[1 + i, k], preferred_element_type=jnp.float32)
+        out_ref[k] = total
     for load in later:
         load.wait()
 
@@ -111,9 +114,12 @@
         out_ref[k] = total
 
 
-def project_far_body(w_ref, block, before_ref, out_ref):
+def project_far_body(w_ref, *refs):
+    blocks, (before_ref, out_ref) = refs[:-2], refs[-2:]
     for k in range(w_ref.shape[1]):
-        total = before_ref[k] + jnp.dot(block[...], w_ref[0, k], preferred_element_type=jnp.float32)
+        total = before_ref[k]
+        for i, block in enumerate(blocks):
+            total = total + jnp.dot(block[...], w_ref[i, k], preferred_element_type=jnp.float32)
         turned = total.T.reshape(out_ref.shape[0], out_ref.shape[2], out_ref.shape[3])
         out_ref[:, k] = turned.astype(jnp.bfloat16)
 
@@ -152,33 +158,30 @@
         out_ref[:, y] = mixed
 
 
-def output_body(index, half_hbm, twin_hbm, mixer_ref, w_ref, *refs):
-    outs, (half_ref, twin_ref, total_ref, sem) = refs[:-4], refs[-4:]
-    loads = [
-        pltpu.make_async_copy(half_hbm, half_ref, sem.at[0]),
-        pltpu.make_async_copy(twin_hbm, twin_ref, sem.at[1]),
-    ]
+def stack_body(half_hbm, twin_hbm, out_ref, sem):
+    half, loads = half_hbm.shape[1], []
+    for i, source in enumerate((half_hbm, twin_hbm)):
+        loads.append(pltpu.make_async_copy(source, out_ref.at[:, pl.ds(i * half, half)], sem.at[i]))
+        loads[-1].start()
     for load in loads:
-        load.start()
+        load.wait()
+
+
+def output_body(index, mixer_ref, w_ref, other_ref, *outs):
     iy, core = index[0], index[1]
     count, _, per, rows = mixer_ref.shape
     half = count // 2
-
-    def mixer_of(block):
-        block = block.astype(jnp.float32)
-        return block.reshape(block.shape[0] * per, rows).T.astype(jnp.bfloat16)
-
-    mine = mixer_of(mixer_ref[:, iy])
-    here = mixer_of(mixer_ref[pl.ds(core * half, half), 1 - iy])
-    there = mixer_of(mixer_ref[pl.ds((1 - core) * half, half), 1 - iy])
-    for i in range(len(outs)):
-        total_ref[i] = jnp.dot(mine, w_ref[index[2 + i]], preferred_element_type=jnp.float32)
-    for load in loads:
-        load.wait()
+    pieces = (
+        mixer_ref[:, iy],
+        mixer_ref[pl.ds(core * half, half), 1 - iy],
+        mixer_ref[pl.ds((1 - core) * half, half), 1 - iy],
+    )
+    turned = [p.astype(jnp.float32).reshape(p.shape[0] * per, rows).T.astype(jnp.bfloat16) for p in pieces]
+    mine, others = turned[0], jnp.concatenate(turned[1:], axis=1)
     for i, out in enumerate(outs):
         x = index[2 + i]
-        total = total_ref[i] + jnp.dot(here, half_ref[x], preferred_element_type=jnp.float32)
-        total = total + jnp.dot(there, twin_ref[x], preferred_element_type=jnp.float32)
+        total = jnp.dot(mine, w_ref[x], preferred_element_type=jnp.float32)
+        total = total + jnp.dot(others, other_ref[x], preferred_element_type=jnp.float32)
         out[...] = total.astype(out.dtype)
 
 
@@ -235,17 +238,27 @@
         vmem=52,
         nbytes=chan_dev * width,
     )
+    order = jnp.concatenate([order[:first], order[first + 1 : first + 3], order[first : first + 1], order[first + 3 :]])
+    w_first = call(
+        fetch_body,
+        shape((first,) + chunk, bf),
+        [order, w3],
+        "sh",
+        scratch=[dma((first,))],
+        vmem=48,
+        nbytes=kinds * feats * chan_dev,
+    )
     acc, w_next = call(
         project_near_body,
         [partial, shape((first,) + chunk, bf)],
-        [order, w3, across] + near,
+        [order, w3, w_first, across] + near,
         "sh",
-        scratch=[pltpu.VMEM((first,) + chunk, bf), dma((first,)), dma((first,))],
-        vmem=48,
+        scratch=[dma((first,))],
+        vmem=46,
         **work,
     )
-    acc = call(functools.partial(project_mid_body, 1), partial, [w_next] + far[1:] + [tokens, acc], "", **work)
-    proj = call(project_far_body, shape((n_seq, kinds, per, rows), bf), [w_next, far[0], acc], "", **work)
+    acc = call(functools.partial(project_mid_body, 2), partial, [w_next, far[0], tokens, acc], "", **work)
+    proj = call(project_far_body, shape((n_seq, kinds, per, rows), bf), [w_next] + far[1:] + [acc], "", **work)
     columns = lax.ppermute(columns, ("yl", "yh"), [(i, 3 - i) for i in range(4)])
     twin = lax.ppermute(columns, "core", [(0, 1), (1, 0)])
     proj = lax.all_to_all(proj, SEQ, 0, 0, tiled=True)
@@ -269,18 +282,20 @@
         scratch=[dma((nx,))],
         nbytes=chan_dev * width,
     )
+    stacked = call(
+        stack_body,
+        shape((nx, chan_dev, feats), bf),
+        [columns, twin],
+        "hh",
+        scratch=[dma((2,))],
+        nbytes=chan_dev * width,
+    )
     block, wide = shape((rows, feats), bf), shape((rows, feats), f32)
     sends = call(
         output_body,
         [block] * (nx - 1) + [wide],
-        [jnp.stack([iy, core] + [x_of(d) for d in steps + [0]]), columns, twin, mixer, own_columns],
-        "shh",
-        scratch=[
-            pltpu.VMEM(columns.shape, bf),
-            pltpu.VMEM(columns.shape, bf),
-            pltpu.VMEM((nx, rows, feats), f32),
-            dma((2,)),
-        ],
+        [jnp.stack([iy, core] + [x_of(d) for d in steps + [0]]), mixer, own_columns, stacked],
+        "s",
         flops=2 * rows * chan_dev * width,
         nbytes=2 * chan_dev * width,
     )

time: 75.3 us -> 74.3 us (0.987)
  waiting for transfers between devices: 30.8 us -> 28.7 us
  Pallas kernels: 11.3 us -> 13 us
    pallas_call x9 -> x11, Pallas kernels: 11.3 us -> 13 us  [call(): pl.pallas_call(body, out_shape=out_shape, in_specs=[pl.BlockSpec(memory_s...]
    ppermute x10, starting transfers between devices: 12.6 us -> 11.3 us  [chan_shift(): return lax.ppermute(block, CHAN, pairs)]
    all_to_all x1, waiting for transfers between devices: 10 us -> 8.78 us  [layer(): mixer = lax.all_to_all(mixer, SEQ + ('yh',), 0, 0, tiled=True)]
    ppermute x10, waiting for transfers between devices: 10.8 us -> 9.95 us  [chan_shift(): return lax.ppermute(block, CHAN, pairs)]
  transfers between devices with their start and end apart: 14 -> 14, of which waited for: 7 -> 7; matrix products, arithmetic and copies ran while one was open for 0% -> 0% of each run, Pallas kernels for 10% -> 14%
where the time goes in v4:
time: 74.3 us; the launch traced here: 73.2 us
  starting transfers between devices  29.2 us (39%)
  waiting for transfers between devices  28.7 us (39%)
  Pallas kernels  13 us (17%)
  local copies, waits for them, and re-layouts  1.15 us (2%)
  other arithmetic  0.88 us (1%)
    pallas_call x11, Pallas kernels, call(): pl.pallas_call(body, out_shape=out_shape, in_specs=[pl.BlockSpec(memory_s...  13 us
    ppermute x10, starting transfers between devices, chan_shift(): return lax.ppermute(block, CHAN, pairs)  11.3 us
    all_to_all x1, waiting for transfers between devices, layer(): proj = lax.all_to_all(proj, SEQ, 0, 0, tiled=True)  10 us
    ppermute x10, waiting for transfers between devices, chan_shift(): return lax.ppermute(block, CHAN, pairs)  9.95 us
    all_to_all x1, starting transfers between devices, layer(): proj = lax.all_to_all(proj, SEQ, 0, 0, tiled=True)  8.85 us
    all_to_all x1, waiting for transfers between devices, layer(): mixer = lax.all_to_all(mixer, SEQ + ('yh',), 0, 0, tiled=True)  8.78 us
    all_to_all x1, starting transfers between devices, layer(): mixer = lax.all_to_all(mixer, SEQ + ('yh',), 0, 0, tiled=True)  5.62 us
    ppermute x1, starting transfers between devices, layer(): lax.ppermute(columns, ('yl', 'yh'), [(i, 3 - i) for i in range(4)])  3.1 us
  transfers between devices with their start and end apart: 14, of which 7 were waited for; matrix products, arithmetic and copies ran while one was open for 0% of the time, Pallas kernels for 14%

profile of v4, /device:TPU:2, one launch (start us, length us, event | category | flops | bytes accessed | tf_op | source)
XLA Modules:
  0.0 73.2 jit_solution(6103095209262062136)
XLA Ops:
  0.1 1.7 %shard_map.72 = bf16[4,128,512]{2,1,0:T(8,128)(2,1)S(1)} custom-call(s32[2]{0:T(128)S(1)} %pad_add_fusion.1.index, bf16[256,4096]{1,0:T(8,128)(2,1)} %w_hbm.3), custom_call_target="tpu_custom_call" | custom-call | flops 1 | bytes 1048576 | tf_op jit(solution)/shard_map/pallas_call | solution.py:30
  1.8 3.1 %collective-permute-start.7 = (bf16[4,128,512]{2,1,0:T(8,128)(2,1)S(1)}, bf16[4,128,512]{2,1,0:T(8,128)(2,1)}, u32[]{:S(2)}, u32[]{:S(2)}) collective-permute-start(bf16[4,128,512]{2,1,0:T(8,128)(2,1)S(1)} %shard_map.72), channel_id=1, source_target_pairs={{0,129},{1,128},{128,1},{129,0},{2,131},{3,130},{130,3},{131,2},{4... | collective-permute-start | bytes 1572872 | tf_op jit(solution)/shard_map/ppermute | solution.py:262
  4.9 2.1 %collective-permute-start.1 = (bf16[128,512]{1,0:T(8,128)(2,1)}, bf16[128,512]{1,0:T(8,128)(2,1)S(1)}, u32[]{:S(2)}, u32[]{:S(2)}) collective-permute-start(bf16[128,512]{1,0:T(8,128)(2,1)} %refs_1_.1), channel_id=1, source_target_pairs={{0,4},{1,5},{2,6},{3,7},{4,0},{5,1},{6,2},{7,3},{8,12},{9,13},{10,... | collective-permute-start | bytes 393224 | tf_op jit(solution)/shard_map/ppermute | solution.py:25
  7.6 2.0 %collective-permute-start.3 = (bf16[128,512]{1,0:T(8,128)(2,1)}, bf16[128,512]{1,0:T(8,128)(2,1)S(1)}, u32[]{:S(2)}, u32[]{:S(2)}) collective-permute-start(bf16[128,512]{1,0:T(8,128)(2,1)} %refs_1_.1), channel_id=1, source_target_pairs={{0,6},{1,7},{2,0},{3,1},{4,2},{5,3},{6,4},{7,5},{8,14},{9,15},{10,... | collective-permute-start | bytes 393224 | tf_op jit(solution)/shard_map/ppermute | solution.py:25
  9.6 2.5 %collective-permute-done.1.refs_1_ = bf16[128,512]{1,0:T(8,128)(2,1)S(1)} collective-permute-done((bf16[128,512]{1,0:T(8,128)(2,1)}, bf16[128,512]{1,0:T(8,128)(2,1)S(1)}, u32[]{:S(2)}, u32[]{:S(2)}) %collective-permute-start.1) | collective-permute-done | bytes 131104 | tf_op jit(solution)/shard_map/ppermute | solution.py:25
  12.5 1.1 %collective-permute-done.refs_0_ = bf16[128,512]{1,0:T(8,128)(2,1)S(1)} collective-permute-done((bf16[128,512]{1,0:T(8,128)(2,1)}, bf16[128,512]{1,0:T(8,128)(2,1)S(1)}, u32[]{:S(2)}, u32[]{:S(2)}) %collective-permute-start) | collective-permute-done | bytes 131104 | tf_op jit(solution)/shard_map/ppermute | solution.py:25
  13.7 0.8 %collective-permute-start.4 = (bf16[128,512]{1,0:T(8,128)(2,1)S(1)}, bf16[128,512]{1,0:T(8,128)(2,1)S(1)}, u32[]{:S(2)}, u32[]{:S(2)}) collective-permute-start(bf16[128,512]{1,0:T(8,128)(2,1)S(1)} %collective-permute-done.refs_0_), channel_id=1, source_target_pairs={{0,2},{1,3},{2,4},{3,5},{4,6},{5,7},{6,0},{7,1},{8,10},{9,11},{10,... | collective-permute-start | bytes 393224 | tf_op jit(solution)/shard_map/ppermute | solution.py:25
  14.4 1.2 %collective-permute-start.5 = (bf16[128,512]{1,0:T(8,128)(2,1)S(1)}, bf16[128,512]{1,0:T(8,128)(2,1)S(1)}, u32[]{:S(2)}, u32[]{:S(2)}) collective-permute-start(bf16[128,512]{1,0:T(8,128)(2,1)S(1)} %collective-permute-done.refs_0_), channel_id=1, source_target_pairs={{0,6},{1,7},{2,0},{3,1},{4,2},{5,3},{6,4},{7,5},{8,14},{9,15},{10,... | collective-permute-start | bytes 393224 | tf_op jit(solution)/shard_map/ppermute | solution.py:25
  15.8 2.4 %shard_map.64.w_ref = bf16[4,3,512,256]{3,2,1,0:T(8,128)(2,1)S(1)} custom-call(s32[8]{0:T(128)S(1)} %concatenate.3.order, bf16[3,8,512,256]{3,2,1,0:T(8,128)(2,1)} %bitcast.24), custom_call_target="tpu_custom_call" | custom-call | flops 1 | bytes 393216 | tf_op jit(solution)/shard_map/pallas_call | solution.py:30
  18.2 2.8 %shard_map.65 = (f32[3,128,256]{2,1,0:T(8,128)S(1)}, bf16[4,3,512,256]{3,2,1,0:T(8,128)(2,1)S(1)}) custom-call(s32[8]{0:T(128)S(1)} %concatenate.3.order, bf16[3,8,512,256]{3,2,1,0:T(8,128)(2,1)} %bitcast.25, bf16[4,3,512,256]{3,2,1,0:T(8,128)(2,1)S(1)} %shard_map.64.w_ref, bf16[128,512]{1,0:T(8,128)(2,1)S(1)} %collective-permute-done.refs_0_, ...), custom_call_target="tpu_custom_call" | custom-call | flops 268435456 | bytes 3145728 | tf_op jit(solution)/shard_map/pallas_call | solution.py:30
  21.5 1.1 %shard_map.67 = bf16[32,3,8,128]{3,2,1,0:T(8,128)(2,1)} custom-call(bf16[4,3,512,256]{3,2,1,0:T(8,128)(2,1)S(1)} %get-tuple-element.13.w_ref, bf16[128,512]{1,0:T(8,128)(2,1)S(1)} %collective-permute-done.4.refs_0_, bf16[128,512]{1,0:T(8,128)(2,1)S(1)} %collective-permute-done.5.refs_1_, f32[3,128,256]{2,1,0:T(8,128)S(1)} %shard_map.66.refs_2_), custom_call_target="tpu_custom_call" | custom-call | flops 268435456 | bytes 3145728 | tf_op jit(solution)/shard_map/pallas_call | solution.py:30
  22.7 8.9 %all-to-all-start = ((bf16[32,3,8,128]{3,2,1,0:T(8,128)(2,1)}), bf16[32,3,8,128]{3,2,1,0:T(8,128)(2,1)S(1)}, u32[]{:S(2)}, u32[]{:S(2)}) async-start(bf16[32,3,8,128]{3,2,1,0:T(8,128)(2,1)} %shard_map.67), calls=%async_computation | async-start | bytes 393216 | tf_op jit(solution)/shard_map/all_to_all | solution.py:264
  32.0 1.0 %copy-done.1 = f32[16,4096]{1,0:T(8,128)S(1)} copy-done((f32[16,4096]{1,0:T(8,128)S(1)}, f32[16,4096]{1,0:T(8,128)}, u32[]{:S(2)}) %copy-start.1) | copy-done | bytes 262168
  33.3 10.0 %all-to-all-done.proj_ref = bf16[32,3,8,128]{3,2,1,0:T(8,128)(2,1)S(1)} async-done(((bf16[32,3,8,128]{3,2,1,0:T(8,128)(2,1)}), bf16[32,3,8,128]{3,2,1,0:T(8,128)(2,1)S(1)}, u32[]{:S(2)}, u32[]{:S(2)}) %all-to-all-start) | async-done | bytes 196640 | tf_op jit(solution)/shard_map/all_to_all | solution.py:264
  43.3 1.2 %shard_map.70 = bf16[32,2,8,128]{3,2,1,0:T(8,128)(2,1)} custom-call(bf16[32,3,8,128]{3,2,1,0:T(8,128)(2,1)S(1)} %all-to-all-done.proj_ref, f32[3,3,8,128]{3,2,1,0:T(8,128)S(1)} %get-tuple-element.15.short_ref, f32[8,128]{1,0:T(8,128)S(1)} %get-tuple-element.16.gain_ref, bf16[4096,128]{1,0:T(8,128)(2,1)S(1)} %shard_map.69.lags_ref), custom_call_target="tpu_custom_call" | custom-call | flops 134217728 | bytes 2097152 | tf_op jit(solution)/shard_map/pallas_call | solution.py:30
  44.5 5.6 %all-to-all-start.1 = ((bf16[64,8,128]{2,1,0:T(8,128)(2,1)}), bf16[64,8,128]{2,1,0:T(8,128)(2,1)S(1)}, u32[]{:S(2)}, u32[]{:S(2)}) async-start(bf16[64,8,128]{2,1,0:T(8,128)(2,1)} %bitcast.19), calls=%async_computation.1 | async-start | bytes 262144 | tf_op jit(solution)/shard_map/all_to_all | solution.py:275
  51.0 1.2 %shard_map.73.other_ref = bf16[4,256,512]{2,1,0:T(8,128)(2,1)S(1)} custom-call(bf16[4,128,512]{2,1,0:T(8,128)(2,1)} %collective-permute-done.7.half_hbm, bf16[4,128,512]{2,1,0:T(8,128)(2,1)} %collective-permute-done.8.twin_hbm), custom_call_target="tpu_custom_call" | custom-call | flops 1 | bytes 1048576 | tf_op jit(solution)/shard_map/pallas_call | solution.py:30
  52.3 8.8 %all-to-all-done.1 = bf16[64,8,128]{2,1,0:T(8,128)(2,1)S(1)} async-done(((bf16[64,8,128]{2,1,0:T(8,128)(2,1)}), bf16[64,8,128]{2,1,0:T(8,128)(2,1)S(1)}, u32[]{:S(2)}, u32[]{:S(2)}) %all-to-all-start.1) | async-done | bytes 131104 | tf_op jit(solution)/shard_map/all_to_all | solution.py:275
  61.0 1.0 %shard_map.74 = (bf16[128,512]{1,0:T(8,128)(2,1)S(1)}, bf16[128,512]{1,0:T(8,128)(2,1)S(1)}, bf16[128,512]{1,0:T(8,128)(2,1)S(1)}, f32[128,512]{1,0:T(8,128)S(1)}) custom-call(s32[6]{0:T(128)S(1)} %stack.56.index, bf16[32,2,8,128]{3,2,1,0:T(8,128)(2,1)S(1)} %bitcast.22, bf16[4,256,512]{2,1,0:T(8,128)(2,1)S(1)} %shard_map.71.w_ref, ...), custom_call_target="tpu_custom_call" | custom-call | flops 268435456 | bytes 2097152 | tf_op jit(solution)/shard_map/pallas_call | solution.py:30
  62.1 1.4 %collective-permute-start.10 = (bf16[128,512]{1,0:T(8,128)(2,1)S(1)}, bf16[128,512]{1,0:T(8,128)(2,1)S(1)}, u32[]{:S(2)}, u32[]{:S(2)}) collective-permute-start(bf16[128,512]{1,0:T(8,128)(2,1)S(1)} %get-tuple-element.19), channel_id=1, source_target_pairs={{0,2},{1,3},{2,4},{3,5},{4,6},{5,7},{6,0},{7,1},{8,10},{9,11},{10,... | collective-permute-start | bytes 393224 | tf_op jit(solution)/shard_map/ppermute | solution.py:25
  63.4 0.7 %collective-permute-start.11 = (bf16[128,512]{1,0:T(8,128)(2,1)S(1)}, bf16[128,512]{1,0:T(8,128)(2,1)S(1)}, u32[]{:S(2)}, u32[]{:S(2)}) collective-permute-start(bf16[128,512]{1,0:T(8,128)(2,1)S(1)} %get-tuple-element.20), channel_id=1, source_target_pairs={{0,6},{1,7},{2,0},{3,1},{4,2},{5,3},{6,4},{7,5},{8,14},{9,15},{10,... | collective-permute-start | bytes 393224 | tf_op jit(solution)/shard_map/ppermute | solution.py:25
  64.2 2.0 %collective-permute-start.9 = (bf16[128,512]{1,0:T(8,128)(2,1)S(1)}, bf16[128,512]{1,0:T(8,128)(2,1)S(1)}, u32[]{:S(2)}, u32[]{:S(2)}) collective-permute-start(bf16[128,512]{1,0:T(8,128)(2,1)S(1)} %get-tuple-element.18), channel_id=1, source_target_pairs={{0,4},{1,5},{2,6},{3,7},{4,0},{5,1},{6,2},{7,3},{8,12},{9,13},{10,... | collective-permute-start | bytes 393224 | tf_op jit(solution)/shard_map/ppermute | solution.py:25
  66.1 1.8 %collective-permute-done.10 = bf16[128,512]{1,0:T(8,128)(2,1)S(1)} collective-permute-done((bf16[128,512]{1,0:T(8,128)(2,1)S(1)}, bf16[128,512]{1,0:T(8,128)(2,1)S(1)}, u32[]{:S(2)}, u32[]{:S(2)}) %collective-permute-start.10) | collective-permute-done | bytes 131104 | tf_op jit(solution)/shard_map/ppermute | solution.py:25
  68.7 3.8 %collective-permute-done.9 = bf16[128,512]{1,0:T(8,128)(2,1)S(1)} collective-permute-done((bf16[128,512]{1,0:T(8,128)(2,1)S(1)}, bf16[128,512]{1,0:T(8,128)(2,1)S(1)}, u32[]{:S(2)}, u32[]{:S(2)}) %collective-permute-start.9) | collective-permute-done | bytes 131104 | tf_op jit(solution)/shard_map/ppermute | solution.py:25
  (30 shorter events, 4.7 us)
Async XLA Ops:
  1.8 29.8 %collective-permute-start.7 = (bf16[4,128,512]{2,1,0:T(8,128)(2,1)S(1)}, bf16[4,128,512]{2,1,0:T(8,128)(2,1)}, u32[]{:S(2)}, u32[]{:S(2)}) collective-permute-start(bf16[4,128,512]{2,1,0:T(8,128)(2,1)S(1)} %shard_map.72), channel_id=1, source_target_pairs={{0,129},{1,128},{128,1},{129,0},{2,131},{3,130},{130,3},{131,2},{4... | collective-permute-start | bytes 1572872 | tf_op jit(solution)/shard_map/ppermute | solution.py:262
  4.9 7.3 %collective-permute-start.1 = (bf16[128,512]{1,0:T(8,128)(2,1)}, bf16[128,512]{1,0:T(8,128)(2,1)S(1)}, u32[]{:S(2)}, u32[]{:S(2)}) collective-permute-start(bf16[128,512]{1,0:T(8,128)(2,1)} %refs_1_.1), channel_id=1, source_target_pairs={{0,4},{1,5},{2,6},{3,7},{4,0},{5,1},{6,2},{7,3},{8,12},{9,13},{10,... | collective-permute-start | bytes 393224 | tf_op jit(solution)/shard_map/ppermute | solution.py:25
  7.0 6.7 %collective-permute-start = (bf16[128,512]{1,0:T(8,128)(2,1)}, bf16[128,512]{1,0:T(8,128)(2,1)S(1)}, u32[]{:S(2)}, u32[]{:S(2)}) collective-permute-start(bf16[128,512]{1,0:T(8,128)(2,1)} %refs_1_.1), channel_id=1, source_target_pairs={{0,1},{1,0},{2,3},{3,2},{4,5},{5,4},{6,7},{7,6},{8,9},{9,8},{10,11... | collective-permute-start | bytes 393224 | tf_op jit(solution)/shard_map/ppermute | solution.py:25
  7.6 6.8 %collective-permute-start.2 = (bf16[128,512]{1,0:T(8,128)(2,1)}, bf16[128,512]{1,0:T(8,128)(2,1)S(1)}, u32[]{:S(2)}, u32[]{:S(2)}) collective-permute-start(bf16[128,512]{1,0:T(8,128)(2,1)} %refs_1_.1), channel_id=1, source_target_pairs={{0,2},{1,3},{2,4},{3,5},{4,6},{5,7},{6,0},{7,1},{8,10},{9,11},{10,... | collective-permute-start | bytes 393224 | tf_op jit(solution)/shard_map/ppermute | solution.py:25
  7.6 10.6 %collective-permute-start.3 = (bf16[128,512]{1,0:T(8,128)(2,1)}, bf16[128,512]{1,0:T(8,128)(2,1)S(1)}, u32[]{:S(2)}, u32[]{:S(2)}) collective-permute-start(bf16[128,512]{1,0:T(8,128)(2,1)} %refs_1_.1), channel_id=1, source_target_pairs={{0,6},{1,7},{2,0},{3,1},{4,2},{5,3},{6,4},{7,5},{8,14},{9,15},{10,... | collective-permute-start | bytes 393224 | tf_op jit(solution)/shard_map/ppermute | solution.py:25
  12.2 8.9 %collective-permute-start.6 = (bf16[128,512]{1,0:T(8,128)(2,1)S(1)}, bf16[128,512]{1,0:T(8,128)(2,1)S(1)}, u32[]{:S(2)}, u32[]{:S(2)}) collective-permute-start(bf16[128,512]{1,0:T(8,128)(2,1)S(1)} %collective-permute-done.1.refs_1_), channel_id=1, source_target_pairs={{0,1},{1,0},{2,3},{3,2},{4,5},{5,4},{6,7},{7,6},{8,9},{9,8},{10,11... | collective-permute-start | bytes 393224 | tf_op jit(solution)/shard_map/ppermute | solution.py:25
  13.7 7.8 %collective-permute-start.4 = (bf16[128,512]{1,0:T(8,128)(2,1)S(1)}, bf16[128,512]{1,0:T(8,128)(2,1)S(1)}, u32[]{:S(2)}, u32[]{:S(2)}) collective-permute-start(bf16[128,512]{1,0:T(8,128)(2,1)S(1)} %collective-permute-done.refs_0_), channel_id=1, source_target_pairs={{0,2},{1,3},{2,4},{3,5},{4,6},{5,7},{6,0},{7,1},{8,10},{9,11},{10,... | collective-permute-start | bytes 393224 | tf_op jit(solution)/shard_map/ppermute | solution.py:25
  14.4 7.1 %collective-permute-start.5 = (bf16[128,512]{1,0:T(8,128)(2,1)S(1)}, bf16[128,512]{1,0:T(8,128)(2,1)S(1)}, u32[]{:S(2)}, u32[]{:S(2)}) collective-permute-start(bf16[128,512]{1,0:T(8,128)(2,1)S(1)} %collective-permute-done.refs_0_), channel_id=1, source_target_pairs={{0,6},{1,7},{2,0},{3,1},{4,2},{5,3},{6,4},{7,5},{8,14},{9,15},{10,... | collective-permute-start | bytes 393224 | tf_op jit(solution)/shard_map/ppermute | solution.py:25
  18.2 2.8 %copy-start.2 = (bf16[128,512]{1,0:T(8,128)(2,1)S(1)}, bf16[128,512]{1,0:T(8,128)(2,1)}, u32[]{:S(2)}) copy-start(bf16[128,512]{1,0:T(8,128)(2,1)} %refs_1_.1) | copy-start | bytes 393220
  21.5 10.4 %copy-start.3 = (f32[3,3,256]{2,1,0:T(4,128)S(1)}, f32[3,3,256]{2,1,0:T(4,128)}, u32[]{:S(2)}) copy-start(f32[3,3,256]{2,1,0:T(4,128)} %taps_ref.1) | copy-start | bytes 27652
  21.5 10.4 %copy-start.4 = (f32[256]{0:T(256)S(1)}, f32[256]{0:T(256)}, u32[]{:S(2)}) copy-start(f32[256]{0:T(256)} %param.9) | copy-start | bytes 3076
  21.5 28.7 %copy-start = (bf16[256,4096]{1,0:T(8,128)(2,1)S(1)}, bf16[256,4096]{1,0:T(8,128)(2,1)}, u32[]{:S(2)}) copy-start(bf16[256,4096]{1,0:T(8,128)(2,1)} %w_hbm.3) | copy-start | bytes 6291460
  22.7 20.6 %all-to-all-start = ((bf16[32,3,8,128]{3,2,1,0:T(8,128)(2,1)}), bf16[32,3,8,128]{3,2,1,0:T(8,128)(2,1)S(1)}, u32[]{:S(2)}, u32[]{:S(2)}) async-start(bf16[32,3,8,128]{3,2,1,0:T(8,128)(2,1)} %shard_map.67), calls=%async_computation | async-start | bytes 393216 | tf_op jit(solution)/shard_map/all_to_all | solution.py:264
  31.5 19.5 %collective-permute-start.8 = (bf16[4,128,512]{2,1,0:T(8,128)(2,1)}, bf16[4,128,512]{2,1,0:T(8,128)(2,1)}, u32[]{:S(2)}, u32[]{:S(2)}) collective-permute-start(bf16[4,128,512]{2,1,0:T(8,128)(2,1)} %collective-permute-done.7.half_hbm), channel_id=1, source_target_pairs={{0,8},{8,0},{1,9},{9,1},{2,10},{10,2},{3,11},{11,3},{4,12},{12,4},... | collective-permute-start | bytes 1572872 | tf_op jit(solution)/shard_map/ppermute | solution.py:263
  32.0 1.0 %copy-start.1 = (f32[16,4096]{1,0:T(8,128)S(1)}, f32[16,4096]{1,0:T(8,128)}, u32[]{:S(2)}) copy-start(f32[16,4096]{1,0:T(8,128)} %filters_ref.1) | copy-start | bytes 786436
  44.5 16.5 %all-to-all-start.1 = ((bf16[64,8,128]{2,1,0:T(8,128)(2,1)}), bf16[64,8,128]{2,1,0:T(8,128)(2,1)S(1)}, u32[]{:S(2)}, u32[]{:S(2)}) async-start(bf16[64,8,128]{2,1,0:T(8,128)(2,1)} %bitcast.19), calls=%async_computation.1 | async-start | bytes 262144 | tf_op jit(solution)/shard_map/all_to_all | solution.py:275
  62.1 5.9 %collective-permute-start.10 = (bf16[128,512]{1,0:T(8,128)(2,1)S(1)}, bf16[128,512]{1,0:T(8,128)(2,1)S(1)}, u32[]{:S(2)}, u32[]{:S(2)}) collective-permute-start(bf16[128,512]{1,0:T(8,128)(2,1)S(1)} %get-tuple-element.19), channel_id=1, source_target_pairs={{0,2},{1,3},{2,4},{3,5},{4,6},{5,7},{6,0},{7,1},{8,10},{9,11},{10,... | collective-permute-start | bytes 393224 | tf_op jit(solution)/shard_map/ppermute | solution.py:25
  63.4 5.2 %collective-permute-start.11 = (bf16[128,512]{1,0:T(8,128)(2,1)S(1)}, bf16[128,512]{1,0:T(8,128)(2,1)S(1)}, u32[]{:S(2)}, u32[]{:S(2)}) collective-permute-start(bf16[128,512]{1,0:T(8,128)(2,1)S(1)} %get-tuple-element.20), channel_id=1, source_target_pairs={{0,6},{1,7},{2,0},{3,1},{4,2},{5,3},{6,4},{7,5},{8,14},{9,15},{10,... | collective-permute-start | bytes 393224 | tf_op jit(solution)/shard_map/ppermute | solution.py:25
  64.2 8.3 %collective-permute-start.9 = (bf16[128,512]{1,0:T(8,128)(2,1)S(1)}, bf16[128,512]{1,0:T(8,128)(2,1)S(1)}, u32[]{:S(2)}, u32[]{:S(2)}) collective-permute-start(bf16[128,512]{1,0:T(8,128)(2,1)S(1)} %get-tuple-element.18), channel_id=1, source_target_pairs={{0,4},{1,5},{2,6},{3,7},{4,0},{5,1},{6,2},{7,3},{8,12},{9,13},{10,... | collective-permute-start | bytes 393224 | tf_op jit(solution)/shard_map/ppermute | solution.py:25

commit v5 on v4

--- a/solution.py
+++ b/solution.py
@@ -88,19 +88,16 @@
         load.wait()
 
 
-def fetch_body(order, w_hbm, out_ref, sem):
-    for load in fetch(order, 0, w_hbm, out_ref, sem):
-        load.wait()
-
-
-def project_near_body(order, w_hbm, w_ref, *refs):
-    blocks, (out_ref, next_ref, next_sem) = refs[:-3], refs[-3:]
-    later = fetch(order, len(blocks), w_hbm, next_ref, next_sem)
-    for k in range(w_ref.shape[1]):
-        total = jnp.dot(blocks[0][...], w_ref[0, k], preferred_element_type=jnp.float32)
-        for i, block in enumerate(blocks[1:]):
-            total = total + jnp.dot(block[...], w_ref[1 + i, k], preferred_element_type=jnp.float32)
-        out_ref[k] = total
+def project_near_body(order, w_hbm, *refs):
+    blocks, (out_ref, next_ref, w_ref, sem, next_sem) = refs[:-5], refs[-5:]
+    count = len(blocks)
+    loads = fetch(order, 0, w_hbm, w_ref, sem)
+    later = fetch(order, count, w_hbm, next_ref, next_sem)
+    for i, block in enumerate(blocks):
+        loads[i].wait()
+        for k in range(w_ref.shape[1]):
+            part = jnp.dot(block[...], w_ref[i, k], preferred_element_type=jnp.float32)
+            out_ref[k] = part if i == 0 else out_ref[k] + part
     for load in later:
         load.wait()
 
@@ -114,12 +111,9 @@
         out_ref[k] = total
 
 
-def project_far_body(w_ref, *refs):
-    blocks, (before_ref, out_ref) = refs[:-2], refs[-2:]
+def project_far_body(w_ref, block, before_ref, out_ref):
     for k in range(w_ref.shape[1]):
-        total = before_ref[k]
-        for i, block in enumerate(blocks):
-            total = total + jnp.dot(block[...], w_ref[i, k], preferred_element_type=jnp.float32)
+        total = before_ref[k] + jnp.dot(block[...], w_ref[0, k], preferred_element_type=jnp.float32)
         turned = total.T.reshape(out_ref.shape[0], out_ref.shape[2], out_ref.shape[3])
         out_ref[:, k] = turned.astype(jnp.bfloat16)
 
@@ -238,27 +232,17 @@
         vmem=52,
         nbytes=chan_dev * width,
     )
-    order = jnp.concatenate([order[:first], order[first + 1 : first + 3], order[first : first + 1], order[first + 3 :]])
-    w_first = call(
-        fetch_body,
-        shape((first,) + chunk, bf),
-        [order, w3],
-        "sh",
-        scratch=[dma((first,))],
-        vmem=48,
-        nbytes=kinds * feats * chan_dev,
-    )
     acc, w_next = call(
         project_near_body,
         [partial, shape((first,) + chunk, bf)],
-        [order, w3, w_first, across] + near,
+        [order, w3, across] + near,
         "sh",
-        scratch=[dma((first,))],
-        vmem=46,
+        scratch=[pltpu.VMEM((first,) + chunk, bf), dma((first,)), dma((first,))],
+        vmem=48,
         **work,
     )
-    acc = call(functools.partial(project_mid_body, 2), partial, [w_next, far[0], tokens, acc], "", **work)
-    proj = call(project_far_body, shape((n_seq, kinds, per, rows), bf), [w_next] + far[1:] + [acc], "", **work)
+    acc = call(functools.partial(project_mid_body, 1), partial, [w_next] + far[1:] + [tokens, acc], "", **work)
+    proj = call(project_far_body, shape((n_seq, kinds, per, rows), bf), [w_next, far[0], acc], "", **work)
     columns = lax.ppermute(columns, ("yl", "yh"), [(i, 3 - i) for i in range(4)])
     twin = lax.ppermute(columns, "core", [(0, 1), (1, 0)])
     proj = lax.all_to_all(proj, SEQ, 0, 0, tiled=True)

time: 74.3 us -> 74.1 us (level)
  Pallas kernels: 13 us -> 11.3 us
  waiting for transfers between devices: 28.7 us -> 29.6 us
    pallas_call x11 -> x10, Pallas kernels: 13 us -> 11.3 us  [call(): pl.pallas_call(body, out_shape=out_shape, in_specs=[pl.BlockSpec(memory_s...]
    ppermute x10, starting transfers between devices: 11.3 us -> 12.6 us  [chan_shift(): return lax.ppermute(block, CHAN, pairs)]
    ppermute x10, waiting for transfers between devices: 9.95 us -> 10.8 us  [chan_shift(): return lax.ppermute(block, CHAN, pairs)]
  transfers between devices with their start and end apart: 14 -> 14, of which waited for: 7 -> 7; matrix products, arithmetic and copies ran while one was open for 0% -> 0% of each run, Pallas kernels for 14% -> 12%
where the time goes in v5:
time: 74.1 us; the launch traced here: 73 us
  starting transfers between devices  29.9 us (40%)
  waiting for transfers between devices  29.6 us (40%)
  Pallas kernels  11.3 us (15%)
  local copies, waits for them, and re-layouts  1.15 us (2%)
  other arithmetic  0.88 us (1%)
    ppermute x10, starting transfers between devices, chan_shift(): return lax.ppermute(block, CHAN, pairs)  12.6 us
    pallas_call x10, Pallas kernels, call(): pl.pallas_call(body, out_shape=out_shape, in_specs=[pl.BlockSpec(memory_s...  11.3 us
    ppermute x10, waiting for transfers between devices, chan_shift(): return lax.ppermute(block, CHAN, pairs)  10.8 us
    all_to_all x1, waiting for transfers between devices, layer(): proj = lax.all_to_all(proj, SEQ, 0, 0, tiled=True)  10 us
    all_to_all x1, starting transfers between devices, layer(): proj = lax.all_to_all(proj, SEQ, 0, 0, tiled=True)  8.86 us
    all_to_all x1, waiting for transfers between devices, layer(): mixer = lax.all_to_all(mixer, SEQ + ('yh',), 0, 0, tiled=True)  8.78 us
    all_to_all x1, starting transfers between devices, layer(): mixer = lax.all_to_all(mixer, SEQ + ('yh',), 0, 0, tiled=True)  5.02 us
    ppermute x1, starting transfers between devices, layer(): lax.ppermute(columns, ('yl', 'yh'), [(i, 3 - i) for i in range(4)])  3.1 us
  transfers between devices with their start and end apart: 14, of which 7 were waited for; matrix products, arithmetic and copies ran while one was open for 0% of the time, Pallas kernels for 12%

profile of v5, /device:TPU:2, one launch (start us, length us, event | category | flops | bytes accessed | tf_op | source)
XLA Modules:
  0.0 73.0 jit_solution(9028891725243931952)
XLA Ops:
  0.1 1.7 %shard_map.71 = bf16[4,128,512]{2,1,0:T(8,128)(2,1)S(1)} custom-call(s32[2]{0:T(128)S(1)} %pad_add_fusion.1.index, bf16[256,4096]{1,0:T(8,128)(2,1)} %w_hbm.3), custom_call_target="tpu_custom_call" | custom-call | flops 1 | bytes 1048576 | tf_op jit(solution)/shard_map/pallas_call | solution.py:30
  1.8 3.1 %collective-permute-start.7 = (bf16[4,128,512]{2,1,0:T(8,128)(2,1)S(1)}, bf16[4,128,512]{2,1,0:T(8,128)(2,1)}, u32[]{:S(2)}, u32[]{:S(2)}) collective-permute-start(bf16[4,128,512]{2,1,0:T(8,128)(2,1)S(1)} %shard_map.71), channel_id=1, source_target_pairs={{0,129},{1,128},{128,1},{129,0},{2,131},{3,130},{130,3},{131,2},{4... | collective-permute-start | bytes 1572872 | tf_op jit(solution)/shard_map/ppermute | solution.py:246
  5.5 2.1 %collective-permute-start.1 = (bf16[128,512]{1,0:T(8,128)(2,1)}, bf16[128,512]{1,0:T(8,128)(2,1)S(1)}, u32[]{:S(2)}, u32[]{:S(2)}) collective-permute-start(bf16[128,512]{1,0:T(8,128)(2,1)} %refs_2_.1), channel_id=1, source_target_pairs={{0,4},{1,5},{2,6},{3,7},{4,0},{5,1},{6,2},{7,3},{8,12},{9,13},{10,... | collective-permute-start | bytes 393224 | tf_op jit(solution)/shard_map/ppermute | solution.py:25
  7.6 2.0 %collective-permute-start.3 = (bf16[128,512]{1,0:T(8,128)(2,1)}, bf16[128,512]{1,0:T(8,128)(2,1)S(1)}, u32[]{:S(2)}, u32[]{:S(2)}) collective-permute-start(bf16[128,512]{1,0:T(8,128)(2,1)} %refs_2_.1), channel_id=1, source_target_pairs={{0,6},{1,7},{2,0},{3,1},{4,2},{5,3},{6,4},{7,5},{8,14},{9,15},{10,... | collective-permute-start | bytes 393224 | tf_op jit(solution)/shard_map/ppermute | solution.py:25
  9.6 2.0 %collective-permute-done.refs_0_ = bf16[128,512]{1,0:T(8,128)(2,1)S(1)} collective-permute-done((bf16[128,512]{1,0:T(8,128)(2,1)}, bf16[128,512]{1,0:T(8,128)(2,1)S(1)}, u32[]{:S(2)}, u32[]{:S(2)}) %collective-permute-start) | collective-permute-done | bytes 131104 | tf_op jit(solution)/shard_map/ppermute | solution.py:25
  11.6 1.5 %collective-permute-start.5 = (bf16[128,512]{1,0:T(8,128)(2,1)S(1)}, bf16[128,512]{1,0:T(8,128)(2,1)S(1)}, u32[]{:S(2)}, u32[]{:S(2)}) collective-permute-start(bf16[128,512]{1,0:T(8,128)(2,1)S(1)} %collective-permute-done.refs_0_), channel_id=1, source_target_pairs={{0,2},{1,3},{2,4},{3,5},{4,6},{5,7},{6,0},{7,1},{8,10},{9,11},{10,... | collective-permute-start | bytes 393224 | tf_op jit(solution)/shard_map/ppermute | solution.py:25
  14.0 2.2 %collective-permute-done.2.refs_2_ = bf16[128,512]{1,0:T(8,128)(2,1)S(1)} collective-permute-done((bf16[128,512]{1,0:T(8,128)(2,1)}, bf16[128,512]{1,0:T(8,128)(2,1)S(1)}, u32[]{:S(2)}, u32[]{:S(2)}) %collective-permute-start.2) | collective-permute-done | bytes 131104 | tf_op jit(solution)/shard_map/ppermute | solution.py:25
  16.2 2.9 %collective-permute-start.4 = (bf16[128,512]{1,0:T(8,128)(2,1)S(1)}, bf16[128,512]{1,0:T(8,128)(2,1)S(1)}, u32[]{:S(2)}, u32[]{:S(2)}) collective-permute-start(bf16[128,512]{1,0:T(8,128)(2,1)S(1)} %collective-permute-done.1.refs_1_), channel_id=1, source_target_pairs={{0,1},{1,0},{2,3},{3,2},{4,5},{5,4},{6,7},{7,6},{8,9},{9,8},{10,11... | collective-permute-start | bytes 393224 | tf_op jit(solution)/shard_map/ppermute | solution.py:25
  19.2 3.5 %shard_map.64 = (f32[3,128,256]{2,1,0:T(8,128)S(1)}, bf16[4,3,512,256]{3,2,1,0:T(8,128)(2,1)S(1)}) custom-call(s32[8]{0:T(128)S(1)} %concatenate.3.order, bf16[3,8,512,256]{3,2,1,0:T(8,128)(2,1)} %bitcast.24, bf16[128,512]{1,0:T(8,128)(2,1)S(1)} %collective-permute-done.refs_0_, bf16[128,512]{1,0:T(8,128)(2,1)S(1)} %collective-permute-done.1.refs_1_, ...), custom_call_target="tpu_custom_call" | custom-call | flops 268435456 | bytes 3145728 | tf_op jit(solution)/shard_map/pallas_call | solution.py:30
  23.2 1.0 %shard_map.66 = bf16[32,3,8,128]{3,2,1,0:T(8,128)(2,1)} custom-call(bf16[4,3,512,256]{3,2,1,0:T(8,128)(2,1)S(1)} %get-tuple-element.13.w_ref, bf16[128,512]{1,0:T(8,128)(2,1)S(1)} %collective-permute-done.4.block, f32[3,128,256]{2,1,0:T(8,128)S(1)} %shard_map.65.before_ref), custom_call_target="tpu_custom_call" | custom-call | flops 268435456 | bytes 3145728 | tf_op jit(solution)/shard_map/pallas_call | solution.py:30
  24.3 8.9 %all-to-all-start = ((bf16[32,3,8,128]{3,2,1,0:T(8,128)(2,1)}), bf16[32,3,8,128]{3,2,1,0:T(8,128)(2,1)S(1)}, u32[]{:S(2)}, u32[]{:S(2)}) async-start(bf16[32,3,8,128]{3,2,1,0:T(8,128)(2,1)} %shard_map.66), calls=%async_computation | async-start | bytes 393216 | tf_op jit(solution)/shard_map/all_to_all | solution.py:248
  33.6 1.0 %copy-done.1 = f32[16,4096]{1,0:T(8,128)S(1)} copy-done((f32[16,4096]{1,0:T(8,128)S(1)}, f32[16,4096]{1,0:T(8,128)}, u32[]{:S(2)}) %copy-start.1) | copy-done | bytes 262168
  34.9 10.0 %all-to-all-done.proj_ref = bf16[32,3,8,128]{3,2,1,0:T(8,128)(2,1)S(1)} async-done(((bf16[32,3,8,128]{3,2,1,0:T(8,128)(2,1)}), bf16[32,3,8,128]{3,2,1,0:T(8,128)(2,1)S(1)}, u32[]{:S(2)}, u32[]{:S(2)}) %all-to-all-start) | async-done | bytes 196640 | tf_op jit(solution)/shard_map/all_to_all | solution.py:248
  44.9 1.2 %shard_map.69 = bf16[32,2,8,128]{3,2,1,0:T(8,128)(2,1)} custom-call(bf16[32,3,8,128]{3,2,1,0:T(8,128)(2,1)S(1)} %all-to-all-done.proj_ref, f32[3,3,8,128]{3,2,1,0:T(8,128)S(1)} %get-tuple-element.15.short_ref, f32[8,128]{1,0:T(8,128)S(1)} %get-tuple-element.16.gain_ref, bf16[4096,128]{1,0:T(8,128)(2,1)S(1)} %shard_map.68.lags_ref), custom_call_target="tpu_custom_call" | custom-call | flops 134217728 | bytes 2097152 | tf_op jit(solution)/shard_map/pallas_call | solution.py:30
  46.1 5.0 %all-to-all-start.1 = ((bf16[64,8,128]{2,1,0:T(8,128)(2,1)}), bf16[64,8,128]{2,1,0:T(8,128)(2,1)S(1)}, u32[]{:S(2)}, u32[]{:S(2)}) async-start(bf16[64,8,128]{2,1,0:T(8,128)(2,1)} %bitcast.18), calls=%async_computation.1 | async-start | bytes 262144 | tf_op jit(solution)/shard_map/all_to_all | solution.py:259
  51.2 0.7 shard_map.70.w_ref
  52.0 1.2 %shard_map.72.other_ref = bf16[4,256,512]{2,1,0:T(8,128)(2,1)S(1)} custom-call(bf16[4,128,512]{2,1,0:T(8,128)(2,1)} %collective-permute-done.7.half_hbm, bf16[4,128,512]{2,1,0:T(8,128)(2,1)} %collective-permute-done.8.twin_hbm), custom_call_target="tpu_custom_call" | custom-call | flops 1 | bytes 1048576 | tf_op jit(solution)/shard_map/pallas_call | solution.py:30
  53.3 8.8 %all-to-all-done.1 = bf16[64,8,128]{2,1,0:T(8,128)(2,1)S(1)} async-done(((bf16[64,8,128]{2,1,0:T(8,128)(2,1)}), bf16[64,8,128]{2,1,0:T(8,128)(2,1)S(1)}, u32[]{:S(2)}, u32[]{:S(2)}) %all-to-all-start.1) | async-done | bytes 131104 | tf_op jit(solution)/shard_map/all_to_all | solution.py:259
  62.1 1.0 %shard_map.73 = (bf16[128,512]{1,0:T(8,128)(2,1)S(1)}, bf16[128,512]{1,0:T(8,128)(2,1)S(1)}, bf16[128,512]{1,0:T(8,128)(2,1)S(1)}, f32[128,512]{1,0:T(8,128)S(1)}) custom-call(s32[6]{0:T(128)S(1)} %stack.56.index, bf16[32,2,8,128]{3,2,1,0:T(8,128)(2,1)S(1)} %bitcast.22, bf16[4,256,512]{2,1,0:T(8,128)(2,1)S(1)} %shard_map.70.w_ref, ...), custom_call_target="tpu_custom_call" | custom-call | flops 268435456 | bytes 2097152 | tf_op jit(solution)/shard_map/pallas_call | solution.py:30
  63.3 1.9 %collective-permute-start.11 = (bf16[128,512]{1,0:T(8,128)(2,1)S(1)}, bf16[128,512]{1,0:T(8,128)(2,1)S(1)}, u32[]{:S(2)}, u32[]{:S(2)}) collective-permute-start(bf16[128,512]{1,0:T(8,128)(2,1)S(1)} %get-tuple-element.20), channel_id=1, source_target_pairs={{0,6},{1,7},{2,0},{3,1},{4,2},{5,3},{6,4},{7,5},{8,14},{9,15},{10,... | collective-permute-start | bytes 393224 | tf_op jit(solution)/shard_map/ppermute | solution.py:25
  65.2 0.7 %collective-permute-start.9 = (bf16[128,512]{1,0:T(8,128)(2,1)S(1)}, bf16[128,512]{1,0:T(8,128)(2,1)S(1)}, u32[]{:S(2)}, u32[]{:S(2)}) collective-permute-start(bf16[128,512]{1,0:T(8,128)(2,1)S(1)} %get-tuple-element.18), channel_id=1, source_target_pairs={{0,4},{1,5},{2,6},{3,7},{4,0},{5,1},{6,2},{7,3},{8,12},{9,13},{10,... | collective-permute-start | bytes 393224 | tf_op jit(solution)/shard_map/ppermute | solution.py:25
  65.9 3.6 %collective-permute-done.10 = bf16[128,512]{1,0:T(8,128)(2,1)S(1)} collective-permute-done((bf16[128,512]{1,0:T(8,128)(2,1)S(1)}, bf16[128,512]{1,0:T(8,128)(2,1)S(1)}, u32[]{:S(2)}, u32[]{:S(2)}) %collective-permute-start.10) | collective-permute-done | bytes 131104 | tf_op jit(solution)/shard_map/ppermute | solution.py:25
  69.5 2.7 %collective-permute-done.9 = bf16[128,512]{1,0:T(8,128)(2,1)S(1)} collective-permute-done((bf16[128,512]{1,0:T(8,128)(2,1)S(1)}, bf16[128,512]{1,0:T(8,128)(2,1)S(1)}, u32[]{:S(2)}, u32[]{:S(2)}) %collective-permute-start.9) | collective-permute-done | bytes 131104 | tf_op jit(solution)/shard_map/ppermute | solution.py:25
  72.2 0.7 add_convert_fusion
  (29 shorter events, 3.3 us)
Async XLA Ops:
  1.8 31.4 %collective-permute-start.7 = (bf16[4,128,512]{2,1,0:T(8,128)(2,1)S(1)}, bf16[4,128,512]{2,1,0:T(8,128)(2,1)}, u32[]{:S(2)}, u32[]{:S(2)}) collective-permute-start(bf16[4,128,512]{2,1,0:T(8,128)(2,1)S(1)} %shard_map.71), channel_id=1, source_target_pairs={{0,129},{1,128},{128,1},{129,0},{2,131},{3,130},{130,3},{131,2},{4... | collective-permute-start | bytes 1572872 | tf_op jit(solution)/shard_map/ppermute | solution.py:246
  4.9 6.8 %collective-permute-start = (bf16[128,512]{1,0:T(8,128)(2,1)}, bf16[128,512]{1,0:T(8,128)(2,1)S(1)}, u32[]{:S(2)}, u32[]{:S(2)}) collective-permute-start(bf16[128,512]{1,0:T(8,128)(2,1)} %refs_2_.1), channel_id=1, source_target_pairs={{0,1},{1,0},{2,3},{3,2},{4,5},{5,4},{6,7},{7,6},{8,9},{9,8},{10,11... | collective-permute-start | bytes 393224 | tf_op jit(solution)/shard_map/ppermute | solution.py:25
  5.5 7.9 %collective-permute-start.1 = (bf16[128,512]{1,0:T(8,128)(2,1)}, bf16[128,512]{1,0:T(8,128)(2,1)S(1)}, u32[]{:S(2)}, u32[]{:S(2)}) collective-permute-start(bf16[128,512]{1,0:T(8,128)(2,1)} %refs_2_.1), channel_id=1, source_target_pairs={{0,4},{1,5},{2,6},{3,7},{4,0},{5,1},{6,2},{7,3},{8,12},{9,13},{10,... | collective-permute-start | bytes 393224 | tf_op jit(solution)/shard_map/ppermute | solution.py:25
  7.6 8.6 %collective-permute-start.2 = (bf16[128,512]{1,0:T(8,128)(2,1)}, bf16[128,512]{1,0:T(8,128)(2,1)S(1)}, u32[]{:S(2)}, u32[]{:S(2)}) collective-permute-start(bf16[128,512]{1,0:T(8,128)(2,1)} %refs_2_.1), channel_id=1, source_target_pairs={{0,2},{1,3},{2,4},{3,5},{4,6},{5,7},{6,0},{7,1},{8,10},{9,11},{10,... | collective-permute-start | bytes 393224 | tf_op jit(solution)/shard_map/ppermute | solution.py:25
  7.6 11.5 %collective-permute-start.3 = (bf16[128,512]{1,0:T(8,128)(2,1)}, bf16[128,512]{1,0:T(8,128)(2,1)S(1)}, u32[]{:S(2)}, u32[]{:S(2)}) collective-permute-start(bf16[128,512]{1,0:T(8,128)(2,1)} %refs_2_.1), channel_id=1, source_target_pairs={{0,6},{1,7},{2,0},{3,1},{4,2},{5,3},{6,4},{7,5},{8,14},{9,15},{10,... | collective-permute-start | bytes 393224 | tf_op jit(solution)/shard_map/ppermute | solution.py:25
  11.6 11.0 %collective-permute-start.5 = (bf16[128,512]{1,0:T(8,128)(2,1)S(1)}, bf16[128,512]{1,0:T(8,128)(2,1)S(1)}, u32[]{:S(2)}, u32[]{:S(2)}) collective-permute-start(bf16[128,512]{1,0:T(8,128)(2,1)S(1)} %collective-permute-done.refs_0_), channel_id=1, source_target_pairs={{0,2},{1,3},{2,4},{3,5},{4,6},{5,7},{6,0},{7,1},{8,10},{9,11},{10,... | collective-permute-start | bytes 393224 | tf_op jit(solution)/shard_map/ppermute | solution.py:25
  13.4 9.3 %collective-permute-start.6 = (bf16[128,512]{1,0:T(8,128)(2,1)S(1)}, bf16[128,512]{1,0:T(8,128)(2,1)S(1)}, u32[]{:S(2)}, u32[]{:S(2)}) collective-permute-start(bf16[128,512]{1,0:T(8,128)(2,1)S(1)} %collective-permute-done.refs_0_), channel_id=1, source_target_pairs={{0,6},{1,7},{2,0},{3,1},{4,2},{5,3},{6,4},{7,5},{8,14},{9,15},{10,... | collective-permute-start | bytes 393224 | tf_op jit(solution)/shard_map/ppermute | solution.py:25
  16.2 7.1 %collective-permute-start.4 = (bf16[128,512]{1,0:T(8,128)(2,1)S(1)}, bf16[128,512]{1,0:T(8,128)(2,1)S(1)}, u32[]{:S(2)}, u32[]{:S(2)}) collective-permute-start(bf16[128,512]{1,0:T(8,128)(2,1)S(1)} %collective-permute-done.1.refs_1_), channel_id=1, source_target_pairs={{0,1},{1,0},{2,3},{3,2},{4,5},{5,4},{6,7},{7,6},{8,9},{9,8},{10,11... | collective-permute-start | bytes 393224 | tf_op jit(solution)/shard_map/ppermute | solution.py:25
  19.2 3.5 %copy-start.2 = (bf16[128,512]{1,0:T(8,128)(2,1)S(1)}, bf16[128,512]{1,0:T(8,128)(2,1)}, u32[]{:S(2)}) copy-start(bf16[128,512]{1,0:T(8,128)(2,1)} %refs_2_.1) | copy-start | bytes 393220
  23.2 10.3 %copy-start.3 = (f32[3,3,256]{2,1,0:T(4,128)S(1)}, f32[3,3,256]{2,1,0:T(4,128)}, u32[]{:S(2)}) copy-start(f32[3,3,256]{2,1,0:T(4,128)} %taps_ref.1) | copy-start | bytes 27652
  23.2 10.3 %copy-start.4 = (f32[256]{0:T(256)S(1)}, f32[256]{0:T(256)}, u32[]{:S(2)}) copy-start(f32[256]{0:T(256)} %param.9) | copy-start | bytes 3076
  23.2 28.0 %copy-start = (bf16[256,4096]{1,0:T(8,128)(2,1)S(1)}, bf16[256,4096]{1,0:T(8,128)(2,1)}, u32[]{:S(2)}) copy-start(bf16[256,4096]{1,0:T(8,128)(2,1)} %w_hbm.3) | copy-start | bytes 6291460
  24.3 20.7 %all-to-all-start = ((bf16[32,3,8,128]{3,2,1,0:T(8,128)(2,1)}), bf16[32,3,8,128]{3,2,1,0:T(8,128)(2,1)S(1)}, u32[]{:S(2)}, u32[]{:S(2)}) async-start(bf16[32,3,8,128]{3,2,1,0:T(8,128)(2,1)} %shard_map.66), calls=%async_computation | async-start | bytes 393216 | tf_op jit(solution)/shard_map/all_to_all | solution.py:248
  33.1 18.9 %collective-permute-start.8 = (bf16[4,128,512]{2,1,0:T(8,128)(2,1)}, bf16[4,128,512]{2,1,0:T(8,128)(2,1)}, u32[]{:S(2)}, u32[]{:S(2)}) collective-permute-start(bf16[4,128,512]{2,1,0:T(8,128)(2,1)} %collective-permute-done.7.half_hbm), channel_id=1, source_target_pairs={{0,8},{8,0},{1,9},{9,1},{2,10},{10,2},{3,11},{11,3},{4,12},{12,4},... | collective-permute-start | bytes 1572872 | tf_op jit(solution)/shard_map/ppermute | solution.py:247
  33.6 1.0 %copy-start.1 = (f32[16,4096]{1,0:T(8,128)S(1)}, f32[16,4096]{1,0:T(8,128)}, u32[]{:S(2)}) copy-start(f32[16,4096]{1,0:T(8,128)} %filters_ref.1) | copy-start | bytes 786436
  46.1 15.9 %all-to-all-start.1 = ((bf16[64,8,128]{2,1,0:T(8,128)(2,1)}), bf16[64,8,128]{2,1,0:T(8,128)(2,1)S(1)}, u32[]{:S(2)}, u32[]{:S(2)}) async-start(bf16[64,8,128]{2,1,0:T(8,128)(2,1)} %bitcast.18), calls=%async_computation.1 | async-start | bytes 262144 | tf_op jit(solution)/shard_map/all_to_all | solution.py:259
  63.1 6.4 %collective-permute-start.10 = (bf16[128,512]{1,0:T(8,128)(2,1)S(1)}, bf16[128,512]{1,0:T(8,128)(2,1)S(1)}, u32[]{:S(2)}, u32[]{:S(2)}) collective-permute-start(bf16[128,512]{1,0:T(8,128)(2,1)S(1)} %get-tuple-element.19), channel_id=1, source_target_pairs={{0,2},{1,3},{2,4},{3,5},{4,6},{5,7},{6,0},{7,1},{8,10},{9,11},{10,... | collective-permute-start | bytes 393224 | tf_op jit(solution)/shard_map/ppermute | solution.py:25
  63.3 6.3 %collective-permute-start.11 = (bf16[128,512]{1,0:T(8,128)(2,1)S(1)}, bf16[128,512]{1,0:T(8,128)(2,1)S(1)}, u32[]{:S(2)}, u32[]{:S(2)}) collective-permute-start(bf16[128,512]{1,0:T(8,128)(2,1)S(1)} %get-tuple-element.20), channel_id=1, source_target_pairs={{0,6},{1,7},{2,0},{3,1},{4,2},{5,3},{6,4},{7,5},{8,14},{9,15},{10,... | collective-permute-start | bytes 393224 | tf_op jit(solution)/shard_map/ppermute | solution.py:25
  65.2 7.0 %collective-permute-start.9 = (bf16[128,512]{1,0:T(8,128)(2,1)S(1)}, bf16[128,512]{1,0:T(8,128)(2,1)S(1)}, u32[]{:S(2)}, u32[]{:S(2)}) collective-permute-start(bf16[128,512]{1,0:T(8,128)(2,1)S(1)} %get-tuple-element.18), channel_id=1, source_target_pairs={{0,4},{1,5},{2,6},{3,7},{4,0},{5,1},{6,2},{7,3},{8,12},{9,13},{10,... | collective-permute-start | bytes 393224 | tf_op jit(solution)/shard_map/ppermute | solution.py:25
